TPU v7x, 128 devices: a whole 4x4x4 slice. The times are simulated.
128 devices in a mesh: lon: 32 (over y, z, x_lo), ch: 4 (over x_hi, core).
Axes of the slice: x: 4 (x_hi: 2, x_lo: 2; x = x_hi * 2 + x_lo), y: 4, z: 4, core: 2. Of those that a mesh axis runs over, the one named last changes fastest.
Arguments:
- features: bfloat16 [1024, 1, 576, 128], P('ch', None, 'lon'), may hold values from -6 to 6
- cotangent: bfloat16 [3, 256, 1, 576, 128], P(None, 'ch', None, 'lon'), may hold values from -6 to 6
- weights: bfloat16 [3, 3, 3, 256, 1024], P(None, None, None, 'ch'), may hold values from -0.0625 to 0.0625
Outputs:
- input_grad: bfloat16 [1024, 1, 576, 128], P('ch', None, 'lon')
- kernel_grad: float32 [3, 3, 3, 256, 1024], P(None, None, None, 'ch')
All inputs are finite; a program needn't handle non-finite values.
Results may differ from a plain program's by a relative error of at most 0.001.
Values may be sent and summed in bfloat16 or wider, within the bound.
A program may use at most 256 MiB of HBM per device.

v0:
```python
import jax
import jax.numpy as jnp
from jax import lax
from jax.sharding import PartitionSpec as P

DILATIONS = (6, 12, 18)
RIM = 18


def with_halo(cells, sides, width):
    for axis, dim in sides:
        count = lax.axis_size(axis)
        head = lax.slice_in_dim(cells, 0, width, axis=dim)
        tail = lax.slice_in_dim(cells, cells.shape[dim] - width, cells.shape[dim], axis=dim)
        cells = jnp.concatenate(
            [
                lax.ppermute(tail, axis, [(i, (i + 1) % count) for i in range(count)]),
                cells,
                lax.ppermute(head, axis, [((i + 1) % count, i) for i in range(count)]),
            ],
            axis=dim,
        )
    return cells


def filter_terms(cotangent, widened):
    lon_cols = cotangent.shape[3]
    lat_rows = cotangent.shape[4]
    padded = jnp.pad(widened, ((0, 0), (0, 0), (0, 0), (RIM, RIM)))
    results = []
    for branch in range(3):
        dilation = DILATIONS[branch]
        for lat_tap in range(3):
            for lon_tap in range(3):
                lon_start = RIM + dilation * (lon_tap - 1)
                lat_start = RIM + dilation * (lat_tap - 1)
                window = padded[
                    :, :, lon_start : lon_start + lon_cols, lat_start : lat_start + lat_rows
                ]
                results.append(
                    lax.dot_general(
                        cotangent[branch],
                        window,
                        (((1, 2, 3), (1, 2, 3)), ((), ())),
                        preferred_element_type=jnp.float32,
                    )
                )
    stacked = jnp.stack(results)
    return stacked.reshape(3, 3, 3, stacked.shape[1], stacked.shape[2])


def branch_taps(grad_ext, offset, dilation, lon_cols, lat_rows):
    grad_pad = jnp.pad(grad_ext, ((0, 0), (0, 0), (0, 0), (dilation, dilation)))
    slices = []
    for lat_tap in range(3):
        for lon_tap in range(3):
            lon_start = offset - dilation * (lon_tap - 1)
            lat_start = dilation - dilation * (lat_tap - 1)
            slices.append(
                grad_pad[:, :, lon_start : lon_start + lon_cols, lat_start : lat_start + lat_rows]
            )
    return jnp.concatenate(slices, axis=0)


def local(features, cotangent, weights):
    in_rows = features.shape[0]
    in_total = weights.shape[4]
    samples = features.shape[1]
    lon_cols = features.shape[2]
    lat_rows = features.shape[3]
    cells_here = samples * lon_cols * lat_rows
    whole = lax.all_gather(features, "ch", axis=0, tiled=True)
    widened = with_halo(whole, (("lon", 2),), RIM)
    partial_kernel = filter_terms(cotangent, widened)
    cells_all = cells_here * lax.axis_size("lon")
    kernel_grad = lax.psum(partial_kernel, "lon") / jnp.sqrt(jnp.float32(cells_all))
    grad_wide = with_halo(cotangent, (("lon", 3),), RIM)
    extended = [grad_wide[0], grad_wide[1], grad_wide[2]]
    offsets = [RIM, RIM, RIM]
    grad_stack = jnp.concatenate(
        [branch_taps(extended[k], offsets[k], DILATIONS[k], lon_cols, lat_rows) for k in range(3)],
        axis=0,
    ).reshape(-1, cells_here)
    kernel_matrix = weights.reshape(-1, in_total)
    product = lax.dot_general(
        kernel_matrix, grad_stack, (((0,), (0,)), ((), ())), preferred_element_type=jnp.float32
    )
    input_grad = lax.psum_scatter(
        product.reshape(lax.axis_size("ch") * in_rows, samples, lon_cols, lat_rows),
        "ch",
        scatter_dimension=0,
        tiled=True,
    ).astype(jnp.bfloat16)
    return (input_grad, kernel_grad)


def solution(mesh):
    return jax.shard_map(
        local,
        mesh=mesh,
        in_specs=(
            P("ch", None, "lon", None),
            P(None, "ch", None, "lon", None),
            P(None, None, None, "ch", None),
        ),
        out_specs=(P("ch", None, "lon", None), P(None, None, None, "ch", None)),
        check_vma=False,
    )
```

profile of v0, /device:TPU:0, one launch (start us, length us, event | category | flops | bytes accessed | tf_op | source)
XLA Modules:
  0.0 891.1 jit_solution(3159787470432086120)
XLA Ops:
  8.0 45.7 %all-gather.2.cloned.1.call-done = bf16[1024,1,18,128]{3,0,2,1:T(8,128)(2,1)} async-done(((bf16[256,1,18,128]{3,0,2,1:T(8,128)(2,1)}), bf16[1024,1,18,128]{3,0,2,1:T(8,128)(2,1)}) %all-gather.2.cloned.1.call-update) | async-done | bytes 4718608 | tf_op jit(solution)/shard_map/all_gather | solution.py:72
  53.7 5.1 collective-permute-start.3
  58.8 6.3 collective-permute-start.1
  65.1 218.1 %collective-permute-done = bf16[3,64,1,18,128]{4,1,3,2,0:T(8,128)(2,1)S(1)} collective-permute-done((bf16[3,64,1,18,128]{4,1,3,2,0:T(8,128)(2,1)}, bf16[3,64,1,18,128]{4,1,3,2,0:T(8,128)(2,1)S(1)}, u32[]{:S(2)}, u32[]{:S(2)}) %collective-permute-start) | collective-permute-done | bytes 884768 | tf_op jit(solution)/shard_map/ppermute | solution.py:17
  283.1 1.1 constant_dynamic-update-slice_fusion.2
  284.2 21.9 %fusion.5 = bf16[1024,1,54,164]{3,0,2,1:T(8,128)(2,1)} fusion(bf16[1024,1,18,128]{3,0,2,1:T(8,128)(2,1)} %collective-permute-done.3, bf16[1024,1,18,128]{3,0,2,1:T(8,128)(2,1)} %all-gather.2.cloned.1.call-done, bf16[1024,1,18,128]{3,0,2,1:T(8,128)(2,1)} %collective-permute-done.2), kind=kLoop, calls=%fused_computation.7 | loop fusion | flops 108822528 | bytes 32292864 | tf_op jit(solution)/shard_map/concatenate | solution.py:15
  306.2 5.9 fusion.69
  312.1 6.0 fusion.71
  318.1 5.9 fusion.73
  323.9 4.8 constant_dynamic-update-slice_fusion.4
  328.8 5.8 constant_dynamic-update-slice_fusion.6
  334.5 4.0 fusion.75
  338.6 1.1 copy-done.3
  339.6 3.0 constant_dynamic-update-slice_fusion.5
  342.7 1.5 fusion.41
  344.2 1.5 fusion.77
  345.7 5.8 fusion.79
  351.6 6.0 fusion.81
  357.6 5.8 fusion.83
  363.4 5.8 fusion.85
  369.2 6.0 fusion.87
  375.2 5.9 fusion.89
  381.1 1.5 fusion.91
  382.6 1.5 fusion.47
  384.2 1.5 fusion.93
  385.7 6.0 fusion.95
  391.7 5.8 fusion.97
  397.6 5.8 fusion.99
  403.4 4.0 fusion.101
  407.4 4.0 fusion.103
  411.4 4.0 fusion.105
  415.5 4.0 fusion.59
  419.5 1.5 fusion.53
  421.0 4.0 fusion.65
  425.1 6.0 fusion.107
  431.1 2.4 fusion.109
  433.5 2.2 fusion.111
  435.7 3.0 copy-done.1
  438.7 2.2 constant_dynamic-update-slice_fusion.1
  440.9 2.3 constant_dynamic-update-slice_fusion
  443.2 2.3 slice_bitcast_fusion.132
  468.6 12.0 %copy.6 = bf16[1728,1,18,128]{0,3,2,1:T(8,128)(2,1)} copy(bf16[1728,1,18,128]{3,0,2,1:T(8,128)(2,1)} %fusion.129) | data formatting | bytes 15925248 | tf_op jit(solution)/shard_map/concatenate | solution.py:80
  480.6 13.2 %fusion.184 = f32[2304,1024]{1,0:T(8,128)} fusion(bf16[1728,2304]{0,1:T(8,128)(2,1)} %bitcast.465, bf16[1728,1024]{1,0:T(8,128)(2,1)S(1)} %bitcast.459), kind=kOutput, calls=%fused_computation.226 | convolution fusion | flops 8153726976 | bytes 20938752 | tf_op jit(solution)/shard_map/dot_general | solution.py:85
  493.8 9.7 %copy.7 = f32[1024,1,18,128]{3,0,2,1:T(8,128)} copy(f32[1024,1,18,128]{0,3,2,1:T(8,128)} %bitcast.464) | data formatting | bytes 18874368 | tf_op jit(solution)/shard_map/reshape | solution.py:89
  503.5 291.5 %all-reduce.6.cloned.1.call-done = f32[3,3,3,64,1024]{4,3,2,1,0:T(8,128)} async-done(((f32[3,3,3,64,1024]{4,3,2,1,0:T(8,128)}), f32[3,3,3,64,1024]{4,3,2,1,0:T(8,128)}) %all-reduce.6.cloned.1.call-update) | async-done | bytes 7077904 | tf_op jit(solution)/shard_map/psum | solution.py:76
  795.0 7.6 broadcast_multiply_fusion
  802.6 78.6 %reduce-scatter.2.cloned.1.call-done = f32[256,1,18,128]{3,0,2,1:T(8,128)} async-done(((f32[1024,1,18,128]{3,0,2,1:T(8,128)}), f32[256,1,18,128]{3,0,2,1:T(8,128)}) %reduce-scatter.2.cloned.1.call-update) | async-done | bytes 2359312 | tf_op jit(solution)/shard_map/reduce_scatter | solution.py:88
  881.2 2.9 convert_element_type.11
  (71 shorter events, 24.1 us)
Async XLA Ops:
  7.2 473.4 %copy-start = (bf16[3,3,3,64,1024]{4,3,2,1,0:T(8,128)(2,1)S(1)}, bf16[3,3,3,64,1024]{4,3,2,1,0:T(8,128)(2,1)}, u32[]{:S(2)}) copy-start(bf16[3,3,3,64,1024]{4,3,2,1,0:T(8,128)(2,1)} %param.5) | copy-start | bytes 10616836
  7.2 46.5 %all-gather.2.cloned.1.call-start = ((), (), s32[]{:S(2)}) async-start(), calls=%async_computation.2 | async-start | bytes 5898240 | tf_op jit(solution)/shard_map/all_gather | solution.py:72
  7.9 787.1 %all-reduce.6.cloned.1.call-start = ((), (), s32[]{:S(2)}) async-start(), calls=%async_computation.3 | async-start | bytes 14155776 | tf_op jit(solution)/shard_map/psum | solution.py:76
  53.7 230.6 %collective-permute-start.3 = (bf16[1024,1,18,128]{3,0,2,1:T(8,128)(2,1)}, bf16[1024,1,18,128]{3,0,2,1:T(8,128)(2,1)}, u32[]{:S(2)}, u32[]{:S(2)}) collective-permute-start(bf16[1024,1,18,128]{3,0,2,1:T(8,128)(2,1)} %all-gather.2.cloned.1.call-done), channel_id=1, source_target_pairs={{4,0},{8,4},{12,8},{16,12},{20,16},{24,20},{28,24},{32,28},{36,32}... | collective-permute-start | bytes 14155784 | tf_op jit(solution)/shard_map/ppermute | solution.py:19
  58.8 225.5 %collective-permute-start.2 = (bf16[1024,1,18,128]{3,0,2,1:T(8,128)(2,1)}, bf16[1024,1,18,128]{3,0,2,1:T(8,128)(2,1)}, u32[]{:S(2)}, u32[]{:S(2)}) collective-permute-start(bf16[1024,1,18,128]{3,0,2,1:T(8,128)(2,1)} %all-gather.2.cloned.1.call-done), channel_id=1, source_target_pairs={{0,4},{4,8},{8,12},{12,16},{16,20},{20,24},{24,28},{28,32},{32,36}... | collective-permute-start | bytes 14155784 | tf_op jit(solution)/shard_map/ppermute | solution.py:17
  58.8 224.4 %collective-permute-start = (bf16[3,64,1,18,128]{4,1,3,2,0:T(8,128)(2,1)}, bf16[3,64,1,18,128]{4,1,3,2,0:T(8,128)(2,1)S(1)}, u32[]{:S(2)}, u32[]{:S(2)}) collective-permute-start(bf16[3,64,1,18,128]{4,1,3,2,0:T(8,128)(2,1)} %param.4), channel_id=1, source_target_pairs={{0,4},{4,8},{8,12},{12,16},{16,20},{20,24},{24,28},{28,32},{32,36}... | collective-permute-start | bytes 2654216 | tf_op jit(solution)/shard_map/ppermute | solution.py:17
  58.8 382.1 %collective-permute-start.1 = (bf16[3,64,1,18,128]{4,1,3,2,0:T(8,128)(2,1)}, bf16[3,64,1,18,128]{4,1,3,2,0:T(8,128)(2,1)}, u32[]{:S(2)}, u32[]{:S(2)}) collective-permute-start(bf16[3,64,1,18,128]{4,1,3,2,0:T(8,128)(2,1)} %param.4), channel_id=1, source_target_pairs={{4,0},{8,4},{12,8},{16,12},{20,16},{24,20},{28,24},{32,28},{36,32}... | collective-permute-start | bytes 2654216 | tf_op jit(solution)/shard_map/ppermute | solution.py:19
  306.2 5.9 copy-start.2
  312.1 16.7 %slice-start = ((s8[4718592]{0:T(1024)(128)(4,1)}), s8[4194304]{0:T(1024)(128)(4,1)S(1)}, s32[]{:S(2)}) async-start(s8[4718592]{0:T(1024)(128)(4,1)} %bitcast.460), calls=%async_computation.4 | async-start | bytes 8388608
  318.0 10.7 %slice-start.1 = ((s8[4718592]{0:T(1024)(128)(4,1)}), s8[524288]{0:T(1024)(128)(4,1)S(1)}, s32[]{:S(2)}) async-start(s8[4718592]{0:T(1024)(128)(4,1)} %bitcast.460), calls=%async_computation.5 | async-start | bytes 1048576
  334.5 5.1 copy-start.3
  369.2 11.9 %slice-start.9 = ((s8[9437184]{0:T(1024)(128)(4,1)}), s8[4194304]{0:T(1024)(128)(4,1)S(1)}, s32[]{:S(2)}) async-start(s8[9437184]{0:T(1024)(128)(4,1)} %bitcast.467), calls=%async_computation.13 | async-start | bytes 8388608
  369.2 11.9 %slice-start.10 = ((s8[9437184]{0:T(1024)(128)(4,1)}), s8[4194304]{0:T(1024)(128)(4,1)S(1)}, s32[]{:S(2)}) async-start(s8[9437184]{0:T(1024)(128)(4,1)} %bitcast.467), calls=%async_computation.14 | async-start | bytes 8388608
  375.2 5.9 slice-start.11
  403.4 27.7 %slice-start.2 = ((s8[28311552]{0:T(1024)(128)(4,1)}), s8[4194304]{0:T(1024)(128)(4,1)S(1)}, s32[]{:S(2)}) async-start(s8[28311552]{0:T(1024)(128)(4,1)} %bitcast.462), calls=%async_computation.6 | async-start | bytes 8388608
  403.4 27.7 %slice-start.3 = ((s8[28311552]{0:T(1024)(128)(4,1)}), s8[4194304]{0:T(1024)(128)(4,1)S(1)}, s32[]{:S(2)}) async-start(s8[28311552]{0:T(1024)(128)(4,1)} %bitcast.462), calls=%async_computation.7 | async-start | bytes 8388608
  407.4 23.6 %slice-start.4 = ((s8[28311552]{0:T(1024)(128)(4,1)}), s8[4194304]{0:T(1024)(128)(4,1)S(1)}, s32[]{:S(2)}) async-start(s8[28311552]{0:T(1024)(128)(4,1)} %bitcast.462), calls=%async_computation.8 | async-start | bytes 8388608
  411.4 19.6 %slice-start.5 = ((s8[28311552]{0:T(1024)(128)(4,1)}), s8[4194304]{0:T(1024)(128)(4,1)S(1)}, s32[]{:S(2)}) async-start(s8[28311552]{0:T(1024)(128)(4,1)} %bitcast.462), calls=%async_computation.9 | async-start | bytes 8388608
  415.5 15.6 %slice-start.6 = ((s8[28311552]{0:T(1024)(128)(4,1)}), s8[4194304]{0:T(1024)(128)(4,1)S(1)}, s32[]{:S(2)}) async-start(s8[28311552]{0:T(1024)(128)(4,1)} %bitcast.462), calls=%async_computation.10 | async-start | bytes 8388608
  421.0 10.1 %slice-start.7 = ((s8[28311552]{0:T(1024)(128)(4,1)}), s8[4194304]{0:T(1024)(128)(4,1)S(1)}, s32[]{:S(2)}) async-start(s8[28311552]{0:T(1024)(128)(4,1)} %bitcast.462), calls=%async_computation.11 | async-start | bytes 8388608
  425.1 6.0 slice-start.8
  435.6 3.0 copy-start.1
  438.6 442.6 %reduce-scatter.2.cloned.1.call-start = ((), (), s32[]{:S(2)}) async-start(), calls=%async_computation.1 | async-start | bytes 11796480 | tf_op jit(solution)/shard_map/reduce_scatter | solution.py:88
Sparse Core Ops, SparseCore 0:
  9.7 43.9 all-gather.1
  438.8 356.1 all-reduce.5
  797.7 83.4 reduce-scatter.1
where the time goes:
time: 896 us; the launch traced here: 891 us
  waiting for transfers between devices  635 us (71%)
  matrix products  128 us (14%)
  local copies, waits for them, and re-layouts  70.4 us (8%)
  other arithmetic  32.5 us (4%)
  between operations  14.5 us (2%)
  starting transfers between devices  11.5 us (1%)
    psum x1, waiting for transfers between devices, local(): lax.psum(partial_kernel, 'lon') / jnp.sqrt(jnp.float32(cells_all))  292 us
    ppermute x2, waiting for transfers between devices, with_halo(): lax.ppermute(tail, axis, [(i, (i + 1) % count) for i in range(count)])  218 us
    dot_general x27, matrix products, filter_terms(): lax.dot_general(cotangent[branch], window, (((1, 2, 3), (1, 2, 3)), ((),...  114 us
    reduce_scatter x1, waiting for transfers between devices, local(): lax.psum_scatter(product.reshape(lax.axis_size('ch') * in_rows, samples,...  78.6 us
    all_gather x1, waiting for transfers between devices, local(): whole = lax.all_gather(features, 'ch', axis=0, tiled=True)  45.7 us
    unnamed x62, local copies, waits for them, and re-layouts  40.3 us
    concatenate x1, other arithmetic, with_halo(): jnp.concatenate([lax.ppermute(tail, axis, [(i, (i + 1) % count) for i in...  21.9 us
  transfers between devices with their start and end apart: 7, of which 4 were waited for; matrix products, arithmetic and copies ran while one was open for 25% of the time, Pallas kernels for 0%

commit v1 on v0

v1 whole, which is shorter than its diff:
```python
import jax
import jax.numpy as jnp
from jax import lax
from jax.experimental import pallas as pl
from jax.experimental.pallas import tpu as pltpu
from jax.sharding import PartitionSpec as P

DILATIONS = (6, 12, 18)


def widened_branches(cotangent):
    count = lax.axis_size("lon")
    cols = cotangent.shape[3]
    tails = jnp.concatenate([cotangent[k, :, 0, cols - d :] for k, d in enumerate(DILATIONS)], axis=1)
    heads = jnp.concatenate([cotangent[k, :, 0, :d] for k, d in enumerate(DILATIONS)], axis=1)
    before = lax.ppermute(tails, "lon", [(i, (i + 1) % count) for i in range(count)])
    after = lax.ppermute(heads, "lon", [((i + 1) % count, i) for i in range(count)])
    wide = []
    start = 0
    for k, d in enumerate(DILATIONS):
        wide.append(
            jnp.concatenate([before[:, start : start + d], cotangent[k, :, 0], after[:, start : start + d]], axis=1)
        )
        start += d
    return wide


def tap_stack(wide, lon_cols, lat_rows):
    slices = []
    for k, d in enumerate(DILATIONS):
        padded = jnp.pad(wide[k], ((0, 0), (0, 0), (d, d)))
        for lat_tap in range(3):
            for lon_tap in range(3):
                lon_start = d - d * (lon_tap - 1)
                lat_start = d - d * (lat_tap - 1)
                slices.append(padded[:, lon_start : lon_start + lon_cols, lat_start : lat_start + lat_rows])
    return jnp.concatenate(slices, axis=0)


MESH = pl.DeviceIdType.MESH
Y, Z, X = 4, 4, 2


def sum_kernel(part, out, acc, first, second, third, low, load_sem, send_sem, recv_sem):
    lon = lax.axis_index("lon")
    ch = lax.axis_index("ch")
    y, z, x = lon // (Z * X), (lon // X) % Z, lon % X
    rows, half = acc.shape[1], acc.shape[2]
    strip = half // 4
    low_rows = rows // 2

    def at(dy, dz, dx):
        place = lax.rem(y + dy, Y) * (Z * X) + lax.rem(z + dz, Z) * X + lax.rem(x + dx, X)
        return (place, ch)

    hops = [(d, 0, 0) for d in (1, 2, 3)], [(0, d, 0) for d in (1, 2, 3)]
    barrier = pltpu.get_barrier_semaphore()
    for hop in hops[0] + hops[1] + [(0, 0, 1)]:
        pl.semaphore_signal(barrier, inc=1, device_id=at(*hop), device_id_type=MESH)
    pl.semaphore_wait(barrier, 7)

    here = (y, z)

    def block(h, row_block):
        return pl.ds(pl.multiple_of(row_block * rows, 8), rows), pl.ds(h * half, half)

    def push(src, dst, slot, hop):
        copy = pltpu.make_async_remote_copy(
            src_ref=src,
            dst_ref=dst,
            send_sem=send_sem.at[slot],
            recv_sem=recv_sem.at[slot],
            device_id=at(*hop),
            device_id_type=MESH,
        )
        copy.start()
        return copy

    stage = [[], []]
    for d in range(3):
        for h in range(2):
            there = block(h, lax.rem(here[h] + d + 1, 4))
            stage[h].append(push(part.at[there], first.at[h, d], h * 3 + d, hops[h][d]))
    loads = []
    for h in range(2):
        load = pltpu.make_async_copy(part.at[block(h, here[h])], acc.at[h], load_sem.at[h])
        load.start()
        loads.append(load)

    def add_first(h):
        def step(i, carry):
            at_rows = pl.ds(pl.multiple_of(i * 16, 16), 16)
            acc[h, at_rows, :] = (acc[h, at_rows, :] + first[h, 0, at_rows, :]) + (
                first[h, 1, at_rows, :] + first[h, 2, at_rows, :]
            )
            return carry

        lax.fori_loop(0, rows // 16, step, 0)

    stage2 = [[], []]
    for h in range(2):
        loads[h].wait()
        for copy in stage[h]:
            copy.wait()
        add_first(h)
        other = here[1 - h]
        for d in range(3):
            cols = pl.ds(pl.multiple_of(lax.rem(other + d + 1, 4) * strip, strip), strip)
            stage2[h].append(push(acc.at[h, :, cols], second.at[h, d], 6 + h * 3 + d, hops[1 - h][d]))

    stage3 = []
    for h in range(2):
        for copy in stage2[h]:
            copy.wait()
        cols = pl.ds(pl.multiple_of(here[1 - h] * strip, strip), strip)

        def step(i, carry):
            at_rows = pl.ds(pl.multiple_of(i * 16, 16), 16)
            second[h, 0, at_rows, :] = (acc[h, at_rows, cols] + second[h, 0, at_rows, :]) + (
                second[h, 1, at_rows, :] + second[h, 2, at_rows, :]
            )
            return carry

        lax.fori_loop(0, rows // 16, step, 0)
        theirs = pl.ds(pl.multiple_of((1 - x) * low_rows, 8), low_rows)
        stage3.append(push(second.at[h, 0, theirs], third.at[h], 12 + h, (0, 0, 1)))

    def corner(h):
        start = here[h] * rows + x * low_rows
        return (
            pl.ds(pl.multiple_of(start, 8), low_rows),
            pl.ds(pl.multiple_of(h * half + here[1 - h] * strip, strip), strip),
        )

    stores, back = [], []
    for h in range(2):
        stage3[h].wait()

        def step(i, carry):
            at_rows = pl.ds(pl.multiple_of(i * 8, 8), 8)
            mine = pl.ds(pl.multiple_of(x * low_rows + i * 8, 8), 8)
            low[h, at_rows, :] = second[h, 0, mine, :] + third[h, at_rows, :]
            return carry

        lax.fori_loop(0, low_rows // 8, step, 0)
        store = pltpu.make_async_copy(low.at[h], out.at[corner(h)], load_sem.at[2 + h])
        store.start()
        stores.append(store)
        back.append(push(low.at[h], out.at[corner(h)], 14 + h, (0, 0, 1)))

    back2 = [[], []]
    for h in range(2):
        stores[h].wait()
        back[h].wait()
        area = (
            pl.ds(pl.multiple_of(here[h] * rows, 8), rows),
            pl.ds(pl.multiple_of(h * half + here[1 - h] * strip, strip), strip),
        )
        for d in range(3):
            back2[h].append(push(out.at[area], out.at[area], 16 + h * 3 + d, hops[1 - h][d]))
    back3 = [[], []]
    for h in range(2):
        for copy in back2[h]:
            copy.wait()
        area = block(h, here[h])
        for d in range(3):
            back3[h].append(push(out.at[area], out.at[area], 22 + h * 3 + d, hops[h][d]))
    for h in range(2):
        for copy in back3[h]:
            copy.wait()


def sum_over_lon(part):
    total, cols = part.shape
    rows, half = total // 4, cols // 2
    return pl.pallas_call(
        sum_kernel,
        out_shape=jax.ShapeDtypeStruct(part.shape, part.dtype),
        in_specs=[pl.BlockSpec(memory_space=pl.ANY)],
        out_specs=pl.BlockSpec(memory_space=pl.ANY),
        scratch_shapes=[
            pltpu.VMEM((2, rows, half), jnp.float32),
            pltpu.VMEM((2, 3, rows, half), jnp.float32),
            pltpu.VMEM((2, 3, rows, half // 4), jnp.float32),
            pltpu.VMEM((2, rows // 2, half // 4), jnp.float32),
            pltpu.VMEM((2, rows // 2, half // 4), jnp.float32),
            pltpu.SemaphoreType.DMA((4,)),
            pltpu.SemaphoreType.DMA((28,)),
            pltpu.SemaphoreType.DMA((28,)),
        ],
        compiler_params=pltpu.CompilerParams(
            collective_id=1, has_side_effects=True, vmem_limit_bytes=24 * 1024 * 1024
        ),
        cost_estimate=pl.CostEstimate(flops=8 * total * cols, bytes_accessed=40 * total * cols * 4, transcendentals=0),
        name="sum_over_lon",
    )(part)


def local(features, cotangent, weights):
    in_rows = features.shape[0]
    in_total = weights.shape[4]
    out_rows = weights.shape[3]
    lon_cols = features.shape[2]
    lat_rows = features.shape[3]
    cells = lon_cols * lat_rows
    whole = lax.all_gather(features, "ch", axis=0, tiled=True).reshape(in_total, cells)
    stack = tap_stack(widened_branches(cotangent), lon_cols, lat_rows).reshape(-1, cells)
    partial_kernel = lax.dot_general(stack, whole, (((1,), (1,)), ((), ())), preferred_element_type=jnp.float32)
    product = lax.dot_general(
        weights.reshape(-1, in_total), stack, (((0,), (0,)), ((), ())), preferred_element_type=jnp.float32
    )
    partial_kernel, product = lax.optimization_barrier((partial_kernel, product))
    input_grad = (
        lax.psum_scatter(product, "ch", scatter_dimension=0, tiled=True)
        .astype(jnp.bfloat16)
        .reshape(in_rows, 1, lon_cols, lat_rows)
    )
    kernel_grad = sum_over_lon(partial_kernel) / jnp.sqrt(jnp.float32(cells * lax.axis_size("lon")))
    kernel_grad = kernel_grad.reshape(3, 3, 3, out_rows, in_total)
    return (input_grad, kernel_grad)


def solution(mesh):
    return jax.shard_map(
        local,
        mesh=mesh,
        in_specs=(
            P("ch", None, "lon", None),
            P(None, "ch", None, "lon", None),
            P(None, None, None, "ch", None),
        ),
        out_specs=(P("ch", None, "lon", None), P(None, None, None, "ch", None)),
        check_vma=False,
    )
```

time: 896 us -> 244 us (0.27)
  waiting for transfers between devices: 635 us -> 30.9 us
  Pallas kernels: 0 us -> 121 us
  matrix products: 128 us -> 25.3 us
  local copies, waits for them, and re-layouts: 70.4 us -> 27.5 us
  other arithmetic: 32.5 us -> 13.2 us
    psum x1 -> x0, waiting for transfers between devices: 292 us -> none  [local(): lax.psum(partial_kernel, 'lon') / jnp.sqrt(jnp.float32(cells_all))]
    ppermute x4 -> x2, waiting for transfers between devices: 218 us -> 30.9 us  [the longest x1 22.8 us: widened_branches(): lax.ppermute(tails, 'lon', [(i, (i + 1) % count) for i in range(count)])]
    pallas_call x0 -> x1, Pallas kernels: none -> 121 us  [sum_over_lon(): pl.pallas_call(sum_kernel, out_shape=jax.ShapeDtypeStruct(part.shape, par...]
    dot_general x28 -> x2, matrix products: 128 us -> 25.3 us  [the longest x1 13.9 us: local(): lax.dot_general(stack, whole, (((1,), (1,)), ((), ())), preferred_element...]
    reduce_scatter x1, waiting for transfers between devices: 78.6 us -> 0.01 us  [local(): lax.psum_scatter(product, 'ch', scatter_dimension=0, tiled=True)]
    all_gather x1, waiting for transfers between devices: 45.7 us -> 0.01 us  [local(): lax.all_gather(features, 'ch', axis=0, tiled=True).reshape(in_total, cells)]
    unnamed x62 -> x45, local copies, waits for them, and re-layouts: 40.3 us -> 15.5 us
    concatenate x4 -> x1, local copies, waits for them, and re-layouts: 18.2 us -> 0.04 us  [tap_stack(): return jnp.concatenate(slices, axis=0)]
  transfers between devices with their start and end apart: 7 -> 4, of which waited for: 4 -> 2; matrix products, arithmetic and copies ran while one was open for 25% -> 15% of each run, Pallas kernels for 0% -> 50%
where the time goes in v1:
time: 244 us; the launch traced here: 240 us
  Pallas kernels  121 us (50%)
  waiting for transfers between devices  30.9 us (13%)
  local copies, waits for them, and re-layouts  27.5 us (11%)
  matrix products  25.3 us (10%)
  between operations  14.4 us (6%)
  other arithmetic  13.2 us (5%)
  starting transfers between devices  7.58 us (3%)
    pallas_call x1, Pallas kernels, sum_over_lon(): pl.pallas_call(sum_kernel, out_shape=jax.ShapeDtypeStruct(part.shape, par...  121 us
    ppermute x1, waiting for transfers between devices, widened_branches(): lax.ppermute(tails, 'lon', [(i, (i + 1) % count) for i in range(count)])  22.8 us
    unnamed x45, local copies, waits for them, and re-layouts  15.5 us
    dot_general x1, matrix products, local(): lax.dot_general(stack, whole, (((1,), (1,)), ((), ())), preferred_element...  13.9 us
    dot_general x1, matrix products, local(): lax.dot_general(weights.reshape(-1, in_total), stack, (((0,), (0,)), ((),...  11.4 us
    ppermute x1, waiting for transfers between devices, widened_branches(): lax.ppermute(heads, 'lon', [((i + 1) % count, i) for i in range(count)])  8.1 us
    ppermute x1, starting transfers between devices, widened_branches(): lax.ppermute(heads, 'lon', [((i + 1) % count, i) for i in range(count)])  7.5 us
  transfers between devices with their start and end apart: 4, of which 2 were waited for; matrix products, arithmetic and copies ran while one was open for 15% of the time, Pallas kernels for 50%

profile of v1, /device:TPU:0, one launch (start us, length us, event | category | flops | bytes accessed | tf_op | source)
XLA Modules:
  0.0 239.8 jit_solution(9713557137086986352)
XLA Ops:
  7.2 0.0 copy-start
  7.2 0.0 all-gather.2.cloned.1.call-start
  7.2 2.7 %fusion.22 = (bf16[1,64,1,18,128]{4,1,3,2,0:T(8,128)(2,1)}, bf16[64,18,128]{2,0,1:T(8,128)(2,1)S(1)}, bf16[64,18,128]{2,0,1:T(8,128)(2,1)}, bf16[64,18,128]{2,0,...) fusion(bf16[3,64,1,18,128]{4,1,3,2,0:T(8,128)(2,1)} %param.4), kind=kLoop, calls=%fused_computation.90 | loop fusion | bytes 2654208 | tf_op jit(solution)/shard_map/slice | solution.py:14
  9.9 0.0 copy-start.3
  9.9 1.2 slice_bitcast_fusion.19
  11.0 1.0 slice_bitcast_fusion.21
  12.0 0.0 copy-done.3
  12.0 1.1 pad_maximum_fusion.1
  13.2 7.5 %collective-permute-start.1 = (bf16[64,36,128]{2,0,1:T(8,128)(2,1)}, bf16[64,36,128]{2,0,1:T(8,128)(2,1)}, u32[]{:S(2)}, u32[]{:S(2)}) collective-permute-start(bf16[64,36,128]{2,0,1:T(8,128)(2,1)} %get-tuple-element.47), channel_id=1, source_target_pairs={{4,0},{8,4},{12,8},{16,12},{20,16},{24,20},{28,24},{32,28},{36,32}... | collective-permute-start | bytes 1769480 | tf_op jit(solution)/shard_map/ppermute | solution.py:17
  20.7 0.0 collective-permute-start
  20.7 2.4 copy.33
  23.0 0.0 all-gather.2.cloned.1.call-update
  23.1 0.0 reduce-scatter.2.cloned.1.call-start
  23.1 1.2 copy.10
  24.3 1.2 copy.19
  25.4 1.2 copy.28
  26.6 8.1 %collective-permute-done.1 = bf16[64,36,128]{2,0,1:T(8,128)(2,1)} collective-permute-done((bf16[64,36,128]{2,0,1:T(8,128)(2,1)}, bf16[64,36,128]{2,0,1:T(8,128)(2,1)}, u32[]{:S(2)}, u32[]{:S(2)}) %collective-permute-start.1) | collective-permute-done | bytes 589856 | tf_op jit(solution)/shard_map/ppermute | solution.py:17
  34.7 0.9 slice.161
  35.6 22.8 %collective-permute-done = bf16[64,36,128]{2,0,1:T(8,128)(2,1)} collective-permute-done((bf16[64,36,128]{2,0,1:T(8,128)(2,1)}, bf16[64,36,128]{2,0,1:T(8,128)(2,1)}, u32[]{:S(2)}, u32[]{:S(2)}) %collective-permute-start) | collective-permute-done | bytes 589856 | tf_op jit(solution)/shard_map/ppermute | solution.py:16
  58.5 0.9 slice.160
  59.4 0.0 copy-start.4
  59.4 1.5 fusion.17
  60.9 0.9 slice.168
  61.8 0.9 slice.169
  62.7 1.3 fusion.18
  64.1 1.7 fusion.12
  65.7 0.5 slice_bitcast_fusion.12
  66.3 0.5 slice_bitcast_fusion.6
  66.8 1.1 slice_bitcast_fusion.22
  67.9 1.1 slice_bitcast_fusion.23
  69.0 0.0 copy-done.4
  69.0 1.0 fusion.7
  70.0 0.5 slice_bitcast_fusion
  71.6 0.0 copy-done
  71.6 0.0 copy-start.5
  71.6 3.2 %copy-done.5 = bf16[1728,2304]{1,0:T(8,128)(2,1)} copy-done((bf16[1728,2304]{1,0:T(8,128)(2,1)}, bf16[1728,2304]{1,0:T(8,128)(2,1)S(1)}, u32[]{:S(2)}) %copy-start.5) | copy-done | bytes 7962648
  74.7 11.4 %convolution_bitcast_fusion = f32[1024,2304]{0,1:T(8,128)} fusion(bf16[1728,2304]{1,0:T(8,128)(2,1)S(1)} %bitcast_dynamic-update-slice_fusion.3, bf16[1728,1024]{1,0:T(8,128)(2,1)S(1)} %bitcast.135), kind=kOutput, calls=%fused_computation | convolution fusion | flops 8153726976 | bytes 20938752 | tf_op jit(solution)/shard_map/dot_general | solution.py:209
  86.2 0.0 all-gather.2.cloned.1.call-done
  86.2 13.9 %fusion.23.part = f32[1728,1024]{1,0:T(8,128)} fusion(bf16[1728,2304]{1,0:T(8,128)(2,1)} %copy-done.5, bf16[1024,2304]{0,1:T(8,128)(2,1)} %bitcast.141), kind=kOutput, calls=%fused_computation.91 | convolution fusion | flops 8153726976 | bytes 19759104 | tf_op jit(solution)/shard_map/dot_general | solution.py:208
  100.1 0.0 reduce-scatter.2.cloned.1.call-update
  100.1 0.0 copy-start.2
  100.1 3.0 %copy-done.2 = f32[1728,1024]{1,0:T(8,128)S(1)} copy-done((f32[1728,1024]{1,0:T(8,128)S(1)}, f32[1728,1024]{1,0:T(8,128)}, u32[]{:S(2)}) %copy-start.2) | copy-done | bytes 7077912
  103.1 0.0 copy-start.1
  103.1 120.9 %sum_over_lon.1 = f32[1728,1024]{1,0:T(8,128)S(1)} custom-call(f32[1728,1024]{1,0:T(8,128)S(1)} %copy-done.2), custom_call_target="tpu_custom_call" | custom-call | flops 14155776 | bytes 283115520 | tf_op jit(solution)/shard_map/sum_over_lon/pallas_call | solution.py:176
  224.0 3.8 %broadcast_multiply_fusion = f32[1728,1024]{1,0:T(8,128)} fusion(f32[1728,1024]{1,0:T(8,128)S(1)} %sum_over_lon.1), kind=kLoop, calls=%fused_computation.5 | loop fusion | flops 1769472 | bytes 14155776 | tf_op jit(solution)/shard_map/div | solution.py:218
  227.8 2.8 %convert_element_type.9 = bf16[256,2304]{0,1:T(8,128)(2,1)} convert(f32[256,2304]{0,1:T(8,128)} %reduce-scatter.2.cloned.1.call-done) | non-fusion elementwise | flops 589824 | bytes 3538944 | tf_op jit(solution)/shard_map/convert_element_type | solution.py:215
  230.6 2.4 copy.34
  233.0 0.0 copy-done.1
  (28 shorter events, 0.9 us)
Async XLA Ops:
  7.2 64.4 %copy-start = (bf16[3,3,3,64,1024]{4,3,2,1,0:T(8,128)(2,1)S(1)}, bf16[3,3,3,64,1024]{4,3,2,1,0:T(8,128)(2,1)}, u32[]{:S(2)}) copy-start(bf16[3,3,3,64,1024]{4,3,2,1,0:T(8,128)(2,1)} %param.5) | copy-start | bytes 10616836
  7.2 79.0 %all-gather.2.cloned.1.call-start = ((), (), s32[]{:S(2)}) async-start(), calls=%async_computation.1 | async-start | bytes 5898240 | tf_op jit(solution)/shard_map/all_gather | solution.py:206
  9.9 2.1 copy-start.3
  13.2 21.5 %collective-permute-start.1 = (bf16[64,36,128]{2,0,1:T(8,128)(2,1)}, bf16[64,36,128]{2,0,1:T(8,128)(2,1)}, u32[]{:S(2)}, u32[]{:S(2)}) collective-permute-start(bf16[64,36,128]{2,0,1:T(8,128)(2,1)} %get-tuple-element.47), channel_id=1, source_target_pairs={{4,0},{8,4},{12,8},{16,12},{20,16},{24,20},{28,24},{32,28},{36,32}... | collective-permute-start | bytes 1769480 | tf_op jit(solution)/shard_map/ppermute | solution.py:17
  20.7 37.8 %collective-permute-start = (bf16[64,36,128]{2,0,1:T(8,128)(2,1)}, bf16[64,36,128]{2,0,1:T(8,128)(2,1)}, u32[]{:S(2)}, u32[]{:S(2)}) collective-permute-start(bf16[64,36,128]{2,0,1:T(8,128)(2,1)} %get-tuple-element.46), channel_id=1, source_target_pairs={{0,4},{4,8},{8,12},{12,16},{16,20},{20,24},{24,28},{28,32},{32,36}... | collective-permute-start | bytes 1769480 | tf_op jit(solution)/shard_map/ppermute | solution.py:16
  23.1 204.7 %reduce-scatter.2.cloned.1.call-start = ((), (), s32[]{:S(2)}) async-start(), calls=%async_computation.2 | async-start | bytes 11796480 | tf_op jit(solution)/shard_map/reduce_scatter | solution.py:214
  59.4 9.6 %copy-start.4 = (bf16[64,18,128]{2,0,1:T(8,128)(2,1)S(1)}, bf16[64,18,128]{2,0,1:T(8,128)(2,1)}, u32[]{:S(2)}) copy-start(bf16[64,18,128]{2,0,1:T(8,128)(2,1)} %copy-done.3) | copy-start | bytes 884740
  71.6 3.2 %copy-start.5 = (bf16[1728,2304]{1,0:T(8,128)(2,1)}, bf16[1728,2304]{1,0:T(8,128)(2,1)S(1)}, u32[]{:S(2)}) copy-start(bf16[1728,2304]{1,0:T(8,128)(2,1)S(1)} %bitcast_dynamic-update-slice_fusion.3) | copy-start | bytes 23887876
  100.1 3.0 %copy-start.2 = (f32[1728,1024]{1,0:T(8,128)S(1)}, f32[1728,1024]{1,0:T(8,128)}, u32[]{:S(2)}) copy-start(f32[1728,1024]{1,0:T(8,128)} %fusion.23.part) | copy-start | bytes 21233668
  103.1 129.9 %copy-start.1 = (bf16[3,3,3,64,1024]{4,3,2,1,0:T(8,128)(2,1)S(1)}, bf16[3,3,3,64,1024]{4,3,2,1,0:T(8,128)(2,1)}, u32[]{:S(2)}) copy-start(bf16[3,3,3,64,1024]{4,3,2,1,0:T(8,128)(2,1)} %param.5) | copy-start | bytes 10616836
Sparse Core Ops, SparseCore 0:
  23.2 53.5 all-gather.1
  100.2 91.2 reduce-scatter.1

commit v2 on v0

v2 whole, which is shorter than its diff:
```python
import functools
import math

import jax
import jax.numpy as jnp
from jax import lax
from jax.experimental import pallas as pl
from jax.experimental.pallas import tpu as pltpu
from jax.sharding import PartitionSpec as P

DILATIONS = (6, 12, 18)
BASES = (0, 30, 72)
MESH = pl.DeviceIdType.MESH
Y, Z, X = 4, 4, 2
CHUNKS = 6


def mod4(v):
    return lax.rem(v, 4)


def aligned(v, m, size):
    return pl.ds(pl.multiple_of(v, m), size)


def backward_kernel(
    scale, feat_hbm, cot_hbm, w_hbm, ig_hbm, kg_hbm,
    ext, stack, raw, flat, wv, wt, part, first, second, low, third, fin, prod, other, across, ig,
    load_sem, halo_send, halo_recv, feat_send, feat_recv, sum_send, sum_recv, ig_send, ig_recv,
):
    lon = lax.axis_index("lon")
    ch = lax.axis_index("ch")
    lons = Y * Z * X
    y, z, x = lon // (Z * X), lax.rem(lon // X, Z), lax.rem(lon, X)
    xh, core = ch // 2, lax.rem(ch, 2)
    cols = feat_hbm.shape[0]
    in_rows = feat_hbm.shape[1]
    out_rows = cot_hbm.shape[2]
    taps = 9 * out_rows
    rows = taps // 4
    here = (y, z)

    def at(dy, dz, dx):
        return (mod4(y + dy) * (Z * X) + mod4(z + dz) * X + lax.rem(x + dx, X), ch)

    hops = [(d, 0, 0) for d in (1, 2, 3)], [(0, d, 0) for d in (1, 2, 3)]
    right = (lax.rem(lon + 1, lons), ch)
    left = (lax.rem(lon + lons - 1, lons), ch)
    mate = (lon, xh * 2 + 1 - core)
    far = (lon, (1 - xh) * 2 + core)

    load_w = pltpu.make_async_copy(w_hbm, wv.at[pl.ds(0, 3 * taps)], load_sem.at[0])
    load_f = pltpu.make_async_copy(feat_hbm, raw.at[ch], load_sem.at[1])
    loads = [
        pltpu.make_async_copy(cot_hbm.at[k], ext.at[pl.ds(BASES[k] + d, cols)], load_sem.at[2 + k])
        for k, d in enumerate(DILATIONS)
    ]
    for copy in loads:
        copy.start()
    load_f.start()
    load_w.start()

    barrier = pltpu.get_barrier_semaphore()
    peers = [at(*hop) for hop in hops[0] + hops[1] + [(0, 0, 1)]] + [right, left, mate, far]
    for peer in peers:
        pl.semaphore_signal(barrier, inc=1, device_id=peer, device_id_type=MESH)
    pl.semaphore_wait(barrier, len(peers))

    def remote(src, dst, send, recv, peer):
        return pltpu.make_async_remote_copy(
            src_ref=src, dst_ref=dst, send_sem=send, recv_sem=recv, device_id=peer, device_id_type=MESH
        )

    halos = []
    for k, d in enumerate(DILATIONS):
        to_right = remote(
            cot_hbm.at[k, pl.ds(cols - d, d)], ext.at[pl.ds(BASES[k], d)], halo_send.at[2 * k], halo_recv.at[2 * k], right
        )
        to_left = remote(
            cot_hbm.at[k, pl.ds(0, d)],
            ext.at[pl.ds(BASES[k] + d + cols, d)],
            halo_send.at[2 * k + 1],
            halo_recv.at[2 * k + 1],
            left,
        )
        to_right.start()
        to_left.start()
        halos.append((to_right, to_left))
    feat_mate = remote(feat_hbm, raw.at[ch], feat_send.at[0], feat_recv.at[0], mate)
    feat_far = remote(feat_hbm, raw.at[ch], feat_send.at[1], feat_recv.at[1], far)
    far_ch = (1 - xh) * 2 + core
    feat_on = remote(raw.at[far_ch], raw.at[far_ch], feat_send.at[2], feat_recv.at[2], mate)
    feat_mate.start()
    feat_far.start()

    lane = lax.broadcasted_iota(jnp.int32, (out_rows, 128), 1)

    def build(k):
        d, base = DILATIONS[k], BASES[k]

        def column(m, carry):
            for lon_tap in range(3):
                v = ext[base + d + m - d * (lon_tap - 1)].astype(jnp.float32)
                for lat_tap in range(3):
                    if lat_tap == 0:
                        moved = jnp.where(lane < 128 - d, pltpu.roll(v, 128 - d, 1), 0.0)
                    elif lat_tap == 1:
                        moved = v
                    else:
                        moved = jnp.where(lane >= d, pltpu.roll(v, d, 1), 0.0)
                    row = k * taps + (lat_tap * 3 + lon_tap) * out_rows
                    stack[pl.ds(row, out_rows), aligned(m * 128, 128, 128)] = moved.astype(jnp.bfloat16)
            return carry

        lax.fori_loop(0, cols, column, 0)

    def flatten(pair):
        def column(m, carry):
            for jj in range(2):
                flat[pl.ds(jj * in_rows, in_rows), aligned(m * 128, 128, 128)] = raw[pair * 2 + jj, m]
            return carry

        lax.fori_loop(0, cols, column, 0)

    def rs1(e, h):
        out = []
        for d in range(3):
            there = mod4(here[h] + d + 1)
            slot = h * 3 + d
            out.append(
                remote(
                    part.at[e, aligned(there * rows, 8, rows), pl.ds(h * 256, 256)],
                    first.at[e, h, d],
                    sum_send.at[e, slot],
                    sum_recv.at[e, slot],
                    at(*hops[h][d]),
                )
            )
        return out

    def piece(h, q, base_row=0, base_col=0):
        return (
            aligned(base_row + here[h] * rows + (q // 2) * (rows // 2), 8, rows // 2),
            aligned(base_col + h * 256 + lax.rem(q, 2) * 128, 128, 128),
        )

    def rs2(e, h):
        out = []
        for d in range(3):
            q = mod4(here[1 - h] + d + 1)
            slot = 6 + h * 3 + d
            r, c = piece(h, q)
            out.append(
                remote(part.at[e, r, c], second.at[e, h, d], sum_send.at[e, slot], sum_recv.at[e, slot], at(*hops[1 - h][d]))
            )
        return out

    def swap(e, h):
        return remote(low.at[e, h], third.at[e, h], sum_send.at[e, 12 + h], sum_recv.at[e, 12 + h], at(0, 0, 1))

    def corner(e):
        pair = jnp.where(e < 3, xh, 1 - xh)
        return lax.rem(e, 3) * taps, pair * 512

    def ag2_local(e, h):
        r, c = piece(h, here[1 - h], *corner(e))
        return pltpu.make_async_copy(fin.at[e, h], kg_hbm.at[r, c], load_sem.at[5 + 2 * e + h])

    def ag2(e, h):
        r, c = piece(h, here[1 - h], *corner(e))
        return [
            remote(
                fin.at[e, h], kg_hbm.at[r, c], sum_send.at[e, 14 + h * 3 + d], sum_recv.at[e, 14 + h * 3 + d], at(*hops[1 - h][d])
            )
            for d in range(3)
        ]

    def ag1(e, h):
        base_row, base_col = corner(e)
        area = kg_hbm.at[
            aligned(base_row + here[h] * rows, 8, rows), aligned(base_col + h * 256, 128, 256)
        ]
        return [
            remote(area, area, sum_send.at[e, 20 + h * 3 + d], sum_recv.at[e, 20 + h * 3 + d], at(*hops[h][d]))
            for d in range(3)
        ]

    def do_chunk(e):
        k = lax.rem(e, 3)
        for h in range(2):
            part[e, :, pl.ds(h * 256, 256)] = lax.dot_general(
                stack[aligned(k * taps, 16, taps), :],
                flat[pl.ds(h * 256, 256), :],
                (((1,), (1,)), ((), ())),
                preferred_element_type=jnp.float32,
            )
            for copy in rs1(e, h):
                copy.start()

    def do_rs2(e):
        for h in range(2):
            for copy in rs1(e, h):
                copy.wait()

            def step(i, carry):
                r = aligned(i * 16, 16, 16)
                mine = aligned(here[h] * rows + i * 16, 8, 16)
                part[e, mine, pl.ds(h * 256, 256)] = (part[e, mine, pl.ds(h * 256, 256)] + first[e, h, 0, r, :]) + (
                    first[e, h, 1, r, :] + first[e, h, 2, r, :]
                )
                return carry

            lax.fori_loop(0, rows // 16, step, 0)
            for copy in rs2(e, h):
                copy.start()

    def do_swap(e):
        for h in range(2):
            for copy in rs2(e, h):
                copy.wait()
            r, c = piece(h, here[1 - h])
            low[e, h] = (part[e, r, c] + second[e, h, 0]) + (second[e, h, 1] + second[e, h, 2])
            swap(e, h).start()

    def do_ag2(e):
        for h in range(2):
            swap(e, h).wait()
            fin[e, h] = (low[e, h] + third[e, h]) * scale
            ag2_local(e, h).start()
            for copy in ag2(e, h):
                copy.start()

    def do_ag1(e):
        for h in range(2):
            ag2_local(e, h).wait()
            for copy in ag2(e, h):
                copy.wait()
            for copy in ag1(e, h):
                copy.start()

    def do_end(e):
        for h in range(2):
            for copy in ag1(e, h):
                copy.wait()

    def ig_block(g):
        chip = jnp.where(g < 2, 1 - xh, xh)
        who = jnp.where(lax.rem(g, 2) == 0, 1 - core, core)
        j = chip * 2 + who
        wt[...] = wv[:, aligned(j * in_rows, 128, in_rows)].T

        def tile(m, carry):
            res = jnp.dot(wt[...], stack[:, aligned(m * 256, 256, 256)], preferred_element_type=jnp.float32)
            prod[g, 2 * m] = res[:, :128]
            prod[g, 2 * m + 1] = res[:, 128:]
            return carry

        lax.fori_loop(0, cols // 2, tile, 0)

    def ig_mate(g):
        return remote(prod.at[2 * g], other.at[g], ig_send.at[g], ig_recv.at[g], mate)

    ig_far = remote(prod.at[1], across, ig_send.at[2], ig_recv.at[2], far)

    def add_other(g):
        def column(m, carry):
            prod[2 * g + 1, m] = prod[2 * g + 1, m] + other[g, m]
            return carry

        lax.fori_loop(0, cols, column, 0)

    pad = stack.shape[0] - 3 * taps
    stack[pl.ds(3 * taps, pad), :] = jnp.zeros((pad, stack.shape[1]), stack.dtype)
    wv[pl.ds(3 * taps, pad), :] = jnp.zeros((pad, wv.shape[1]), wv.dtype)

    def body(s, carry):
        for k in range(3):

            @pl.when(s == k)
            def _():
                loads[k].wait()
                for copy in halos[k]:
                    copy.wait()
                build(k)

        @pl.when(s == 0)
        def _():
            load_f.wait()
            feat_mate.wait()
            flatten(xh)

        @pl.when(s == 3)
        def _():
            feat_on.wait()
            flatten(1 - xh)

        @pl.when(s < CHUNKS)
        def _():
            do_chunk(s)

        @pl.when(s == 2)
        def _():
            feat_far.wait()
            feat_on.start()

        @pl.when((s >= 4) & (s < CHUNKS + 4))
        def _():
            do_ag1(s - 4)

        @pl.when((s >= 3) & (s < CHUNKS + 3))
        def _():
            do_ag2(s - 3)

        @pl.when((s >= 2) & (s < CHUNKS + 2))
        def _():
            do_swap(s - 2)

        @pl.when((s >= 1) & (s < CHUNKS + 1))
        def _():
            do_rs2(s - 1)

        @pl.when(s == 2)
        def _():
            load_w.wait()

        @pl.when((s >= 2) & (s < 6))
        def _():
            g = s - 2
            ig_block(g)

            @pl.when(g == 0)
            def _():
                ig_mate(0).start()

            @pl.when(g == 2)
            def _():
                ig_mate(1).start()

            @pl.when(g == 1)
            def _():
                ig_mate(0).wait()
                add_other(0)
                ig_far.start()

            @pl.when(g == 3)
            def _():
                ig_mate(1).wait()
                add_other(1)

        return carry

    lax.fori_loop(0, CHUNKS + 4, body, 0)
    ig_far.wait()

    def column(m, carry):
        ig[m] = (prod[3, m] + across[m]).astype(jnp.bfloat16)
        return carry

    lax.fori_loop(0, cols, column, 0)
    store = pltpu.make_async_copy(ig, ig_hbm, load_sem.at[0])
    store.start()

    def end(e, carry):
        do_end(e)
        return carry

    lax.fori_loop(0, CHUNKS, end, 0)
    store.wait()


def local(features, cotangent, weights):
    in_rows, _, cols, lats = features.shape
    out_rows, in_total = weights.shape[3:]
    cells = cols * lats
    taps = 9 * out_rows
    rows = taps // 4
    depth = -(-3 * taps // 256) * 256
    scale = 1.0 / math.sqrt(cells * lax.axis_size("lon"))
    f32, bf16 = jnp.float32, jnp.bfloat16
    anywhere = pl.BlockSpec(memory_space=pl.ANY)
    ig, kg = pl.pallas_call(
        functools.partial(backward_kernel, scale),
        out_shape=(
            jax.ShapeDtypeStruct((cols, in_rows, lats), bf16),
            jax.ShapeDtypeStruct((3 * taps, in_total), f32),
        ),
        in_specs=[anywhere] * 3,
        out_specs=(anywhere, anywhere),
        scratch_shapes=[
            pltpu.VMEM((126, out_rows, lats), bf16),
            pltpu.VMEM((depth, cells), bf16),
            pltpu.VMEM((4, cols, in_rows, lats), bf16),
            pltpu.VMEM((2 * in_rows, cells), bf16),
            pltpu.VMEM((depth, in_total), bf16),
            pltpu.VMEM((in_rows, depth), bf16),
            pltpu.VMEM((CHUNKS, taps, 512), f32),
            pltpu.VMEM((CHUNKS, 2, 3, rows, 256), f32),
            pltpu.VMEM((CHUNKS, 2, 3, rows // 2, 128), f32),
            pltpu.VMEM((CHUNKS, 2, rows // 2, 128), f32),
            pltpu.VMEM((CHUNKS, 2, rows // 2, 128), f32),
            pltpu.VMEM((CHUNKS, 2, rows // 2, 128), f32),
            pltpu.VMEM((4, cols, in_rows, lats), f32),
            pltpu.VMEM((2, cols, in_rows, lats), f32),
            pltpu.VMEM((cols, in_rows, lats), f32),
            pltpu.VMEM((cols, in_rows, lats), bf16),
            pltpu.SemaphoreType.DMA((5 + 2 * CHUNKS,)),
            pltpu.SemaphoreType.DMA((6,)),
            pltpu.SemaphoreType.DMA((6,)),
            pltpu.SemaphoreType.DMA((3,)),
            pltpu.SemaphoreType.DMA((3,)),
            pltpu.SemaphoreType.DMA((CHUNKS, 26)),
            pltpu.SemaphoreType.DMA((CHUNKS, 26)),
            pltpu.SemaphoreType.DMA((3,)),
            pltpu.SemaphoreType.DMA((3,)),
        ],
        compiler_params=pltpu.CompilerParams(
            collective_id=1, has_side_effects=True, vmem_limit_bytes=60 * 1024 * 1024
        ),
        name="backward",
    )(
        features.reshape(in_rows, cols, lats).transpose(1, 0, 2),
        cotangent.reshape(3, out_rows, cols, lats).transpose(0, 2, 1, 3),
        weights.reshape(3 * taps, in_total),
    )
    input_grad = ig.transpose(1, 0, 2).reshape(in_rows, 1, cols, lats)
    return (input_grad, kg.reshape(3, 3, 3, out_rows, in_total))


def solution(mesh):
    return jax.shard_map(
        local,
        mesh=mesh,
        in_specs=(
            P("ch", None, "lon", None),
            P(None, "ch", None, "lon", None),
            P(None, None, None, "ch", None),
        ),
        out_specs=(P("ch", None, "lon", None), P(None, None, None, "ch", None)),
        check_vma=False,
    )
```

time: 896 us -> 185 us (0.21)
  waiting for transfers between devices: 635 us -> 0 us
  Pallas kernels: 0 us -> 172 us
  matrix products: 128 us -> 0 us
  local copies, waits for them, and re-layouts: 70.4 us -> 9.68 us
  other arithmetic: 32.5 us -> 0 us
  between operations: 14.5 us -> 0.64 us
  starting transfers between devices: 11.5 us -> 0 us
    psum x1 -> x0, waiting for transfers between devices: 292 us -> none  [local(): lax.psum(partial_kernel, 'lon') / jnp.sqrt(jnp.float32(cells_all))]
    ppermute x4 -> x0, waiting for transfers between devices: 218 us -> none  [the longest x2 218 us: with_halo(): lax.ppermute(tail, axis, [(i, (i + 1) % count) for i in range(count)])]
    pallas_call x0 -> x1, Pallas kernels: none -> 172 us  [local(): pl.pallas_call(functools.partial(backward_kernel, scale), out_shape=(jax....]
    dot_general x28 -> x0, matrix products: 128 us -> none  [the longest x27 114 us: filter_terms(): lax.dot_general(cotangent[branch], window, (((1, 2, 3), (1, 2, 3)), ((),...]
    reduce_scatter x1 -> x0, waiting for transfers between devices: 78.6 us -> none  [local(): lax.psum_scatter(product.reshape(lax.axis_size('ch') * in_rows, samples,...]
    all_gather x1 -> x0, waiting for transfers between devices: 45.7 us -> none  [local(): whole = lax.all_gather(features, 'ch', axis=0, tiled=True)]
    unnamed x62 -> x2, local copies, waits for them, and re-layouts: 40.3 us -> 9.68 us
    concatenate x1 -> x0, other arithmetic: 21.9 us -> none  [with_halo(): jnp.concatenate([lax.ppermute(tail, axis, [(i, (i + 1) % count) for i in...]
  transfers between devices with their start and end apart: 7 -> 0, of which waited for: 4 -> 0; matrix products, arithmetic and copies ran while one was open for 25% -> 0% of each run, Pallas kernels for 0% -> 0%
where the time goes in v2:
time: 185 us; the launch traced here: 182 us
  Pallas kernels  172 us (93%)
  local copies, waits for them, and re-layouts  9.68 us (5%)
    pallas_call x1, Pallas kernels, local(): pl.pallas_call(functools.partial(backward_kernel, scale), out_shape=(jax....  172 us
    unnamed x2, local copies, waits for them, and re-layouts  9.68 us

profile of v2, /device:TPU:0, one launch (start us, length us, event | category | flops | bytes accessed | tf_op | source)
XLA Modules:
  0.0 182.5 jit_solution(5322232252876127336)
XLA Ops:
  0.6 172.2 %backward.1 = (bf16[18,256,128]{2,1,0:T(8,128)(2,1)}, f32[1728,1024]{1,0:T(8,128)}) custom-call(bf16[18,256,128]{2,1,0:T(8,128)(2,1)} %bitcast.14, bf16[3,18,64,128]{3,2,1,0:T(8,128)(2,1)} %bitcast.15, bf16[1728,1024]{1,0:T(8,128)(2,1)} %bitcast.12), custom_call_target="tpu_custom_call" | custom-call | tf_op jit(solution)/shard_map/backward/pallas_call | solution.py:381
  172.8 2.4 %copy.7 = bf16[256,1,18,128]{3,0,2,1:T(8,128)(2,1)} copy(bf16[256,1,18,128]{3,0,2,1:T(8,128)(2,1)} %bitcast.13) | data formatting | bytes 2359296
  175.2 7.3 %copy.8 = f32[3,3,3,64,1024]{4,3,2,1,0:T(8,128)} copy(f32[3,3,3,64,1024]{4,3,2,1,0:T(8,128)} %bitcast.11) | data formatting | bytes 14155776

commit v3 on v2

--- a/solution.py
+++ b/solution.py
@@ -9,10 +9,11 @@
 from jax.sharding import PartitionSpec as P
 
 DILATIONS = (6, 12, 18)
-BASES = (0, 30, 72)
+BASES = (0, 48, 108)
 MESH = pl.DeviceIdType.MESH
 Y, Z, X = 4, 4, 2
 CHUNKS = 6
+LAG = (1, 2, 3, 4)
 
 
 def mod4(v):
@@ -44,15 +45,17 @@
         return (mod4(y + dy) * (Z * X) + mod4(z + dz) * X + lax.rem(x + dx, X), ch)
 
     hops = [(d, 0, 0) for d in (1, 2, 3)], [(0, d, 0) for d in (1, 2, 3)]
-    right = (lax.rem(lon + 1, lons), ch)
-    left = (lax.rem(lon + lons - 1, lons), ch)
+    twin = at(0, 0, 1)
+    pair = lon - x
     mate = (lon, xh * 2 + 1 - core)
-    far = (lon, (1 - xh) * 2 + core)
+    far = (pair + 1 - x, (1 - xh) * 2 + core)
+    outer = [(lax.rem(pair + step, lons), ch) for step in (lons - 2, lons - 1, 2, 3)]
+    halo_to = [(lax.rem(pair + lons - 2 + 4 * x + i, lons), ch) for i in range(2)]
 
     load_w = pltpu.make_async_copy(w_hbm, wv.at[pl.ds(0, 3 * taps)], load_sem.at[0])
-    load_f = pltpu.make_async_copy(feat_hbm, raw.at[ch], load_sem.at[1])
+    load_f = pltpu.make_async_copy(feat_hbm, raw.at[core], load_sem.at[1])
     loads = [
-        pltpu.make_async_copy(cot_hbm.at[k], ext.at[pl.ds(BASES[k] + d, cols)], load_sem.at[2 + k])
+        pltpu.make_async_copy(cot_hbm.at[k], ext.at[pl.ds(BASES[k] + d + x * cols, cols)], load_sem.at[2 + k])
         for k, d in enumerate(DILATIONS)
     ]
     for copy in loads:
@@ -61,7 +64,7 @@
     load_w.start()
 
     barrier = pltpu.get_barrier_semaphore()
-    peers = [at(*hop) for hop in hops[0] + hops[1] + [(0, 0, 1)]] + [right, left, mate, far]
+    peers = [at(*hop) for hop in hops[0] + hops[1]] + [twin, mate, far] + outer
     for peer in peers:
         pl.semaphore_signal(barrier, inc=1, device_id=peer, device_id_type=MESH)
     pl.semaphore_wait(barrier, len(peers))
@@ -71,36 +74,45 @@
             src_ref=src, dst_ref=dst, send_sem=send, recv_sem=recv, device_id=peer, device_id_type=MESH
         )
 
-    halos = []
+    inputs = []
     for k, d in enumerate(DILATIONS):
-        to_right = remote(
-            cot_hbm.at[k, pl.ds(cols - d, d)], ext.at[pl.ds(BASES[k], d)], halo_send.at[2 * k], halo_recv.at[2 * k], right
+        base = BASES[k]
+        mine = remote(
+            cot_hbm.at[k], ext.at[pl.ds(base + d + x * cols, cols)], halo_send.at[3 * k], halo_recv.at[3 * k], twin
         )
-        to_left = remote(
-            cot_hbm.at[k, pl.ds(0, d)],
-            ext.at[pl.ds(BASES[k] + d + cols, d)],
-            halo_send.at[2 * k + 1],
-            halo_recv.at[2 * k + 1],
-            left,
-        )
-        to_right.start()
-        to_left.start()
-        halos.append((to_right, to_left))
-    feat_mate = remote(feat_hbm, raw.at[ch], feat_send.at[0], feat_recv.at[0], mate)
-    feat_far = remote(feat_hbm, raw.at[ch], feat_send.at[1], feat_recv.at[1], far)
-    far_ch = (1 - xh) * 2 + core
-    feat_on = remote(raw.at[far_ch], raw.at[far_ch], feat_send.at[2], feat_recv.at[2], mate)
+        edges = [
+            remote(
+                cot_hbm.at[k, pl.ds(x * (cols - d), d)],
+                ext.at[pl.ds(base + (1 - x) * (2 * cols + d), d)],
+                halo_send.at[3 * k + 1 + i],
+                halo_recv.at[3 * k + 1 + (1 - x)],
+                halo_to[i],
+            )
+            for i in range(2)
+        ]
+        for copy in edges + [mine]:
+            copy.start()
+        before = ext.at[pl.ds(base, d)]
+        after = ext.at[pl.ds(base + 2 * cols + d, d)]
+        arrivals = [
+            remote(before, before, halo_send.at[3 * k + 1], halo_recv.at[3 * k + 1], halo_to[0]),
+            remote(after, after, halo_send.at[3 * k + 1], halo_recv.at[3 * k + 2], halo_to[0]),
+        ]
+        inputs.append((mine, edges, arrivals))
+    feat_mate = remote(feat_hbm, raw.at[core], feat_send.at[0], feat_recv.at[0], mate)
+    feat_far = remote(feat_hbm, raw.at[2 + core], feat_send.at[1], feat_recv.at[1], far)
+    feat_on = remote(raw.at[2 + core], raw.at[2 + core], feat_send.at[2], feat_recv.at[2], mate)
     feat_mate.start()
     feat_far.start()
 
     lane = lax.broadcasted_iota(jnp.int32, (out_rows, 128), 1)
 
-    def build(k):
+    def build(k, side):
         d, base = DILATIONS[k], BASES[k]
 
         def column(m, carry):
             for lon_tap in range(3):
-                v = ext[base + d + m - d * (lon_tap - 1)].astype(jnp.float32)
+                v = ext[base + d + side * cols + m - d * (lon_tap - 1)].astype(jnp.float32)
                 for lat_tap in range(3):
                     if lat_tap == 0:
                         moved = jnp.where(lane < 128 - d, pltpu.roll(v, 128 - d, 1), 0.0)
@@ -114,10 +126,10 @@
 
         lax.fori_loop(0, cols, column, 0)
 
-    def flatten(pair):
+    def flatten(chip):
         def column(m, carry):
             for jj in range(2):
-                flat[pl.ds(jj * in_rows, in_rows), aligned(m * 128, 128, 128)] = raw[pair * 2 + jj, m]
+                flat[pl.ds(jj * in_rows, in_rows), aligned(m * 128, 128, 128)] = raw[chip * 2 + jj, m]
             return carry
 
         lax.fori_loop(0, cols, column, 0)
@@ -159,8 +171,8 @@
         return remote(low.at[e, h], third.at[e, h], sum_send.at[e, 12 + h], sum_recv.at[e, 12 + h], at(0, 0, 1))
 
     def corner(e):
-        pair = jnp.where(e < 3, xh, 1 - xh)
-        return lax.rem(e, 3) * taps, pair * 512
+        chip = jnp.where(e < 3, xh, 1 - xh)
+        return lax.rem(e, 3) * taps, chip * 512
 
     def ag2_local(e, h):
         r, c = piece(h, here[1 - h], *corner(e))
@@ -244,7 +256,7 @@
                 copy.wait()
 
     def ig_block(g):
-        chip = jnp.where(g < 2, 1 - xh, xh)
+        chip = jnp.where(g < 2, xh, 1 - xh)
         who = jnp.where(lax.rem(g, 2) == 0, 1 - core, core)
         j = chip * 2 + who
         wt[...] = wv[:, aligned(j * in_rows, 128, in_rows)].T
@@ -260,7 +272,7 @@
     def ig_mate(g):
         return remote(prod.at[2 * g], other.at[g], ig_send.at[g], ig_recv.at[g], mate)
 
-    ig_far = remote(prod.at[1], across, ig_send.at[2], ig_recv.at[2], far)
+    ig_far = remote(prod.at[3], across, ig_send.at[2], ig_recv.at[2], far)
 
     def add_other(g):
         def column(m, carry):
@@ -278,21 +290,27 @@
 
             @pl.when(s == k)
             def _():
+                mine, edges, arrivals = inputs[k]
                 loads[k].wait()
-                for copy in halos[k]:
-                    copy.wait()
-                build(k)
+                mine.wait_recv()
+                for copy in arrivals:
+                    copy.wait_recv()
+                build(k, x)
+
+            @pl.when(s == 3 + k)
+            def _():
+                build(k, 1 - x)
 
         @pl.when(s == 0)
         def _():
             load_f.wait()
             feat_mate.wait()
-            flatten(xh)
+            flatten(0)
 
         @pl.when(s == 3)
         def _():
             feat_on.wait()
-            flatten(1 - xh)
+            flatten(1)
 
         @pl.when(s < CHUNKS)
         def _():
@@ -302,63 +320,47 @@
         def _():
             feat_far.wait()
             feat_on.start()
-
-        @pl.when((s >= 4) & (s < CHUNKS + 4))
-        def _():
-            do_ag1(s - 4)
-
-        @pl.when((s >= 3) & (s < CHUNKS + 3))
-        def _():
-            do_ag2(s - 3)
-
-        @pl.when((s >= 2) & (s < CHUNKS + 2))
-        def _():
-            do_swap(s - 2)
-
-        @pl.when((s >= 1) & (s < CHUNKS + 1))
-        def _():
-            do_rs2(s - 1)
-
-        @pl.when(s == 2)
-        def _():
             load_w.wait()
-
-        @pl.when((s >= 2) & (s < 6))
-        def _():
-            g = s - 2
-            ig_block(g)
-
-            @pl.when(g == 0)
+            ig_block(0)
+            ig_mate(0).start()
+            ig_block(1)
+
+        @pl.when(s == 5)
+        def _():
+            ig_block(2)
+            ig_mate(1).start()
+            ig_block(3)
+
+        @pl.when(s == 6)
+        def _():
+            ig_mate(1).wait()
+            add_other(1)
+            ig_far.start()
+            ig_mate(0).wait()
+            add_other(0)
+
+        for lag, work in zip(LAG[::-1], (do_ag1, do_ag2, do_swap, do_rs2)):
+
+            @pl.when((s >= lag) & (s < CHUNKS + lag))
             def _():
-                ig_mate(0).start()
-
-            @pl.when(g == 2)
-            def _():
-                ig_mate(1).start()
-
-            @pl.when(g == 1)
-            def _():
-                ig_mate(0).wait()
-                add_other(0)
-                ig_far.start()
-
-            @pl.when(g == 3)
-            def _():
-                ig_mate(1).wait()
-                add_other(1)
+                work(s - lag)
 
         return carry
 
-    lax.fori_loop(0, CHUNKS + 4, body, 0)
+    lax.fori_loop(0, CHUNKS + LAG[3], body, 0)
     ig_far.wait()
 
     def column(m, carry):
-        ig[m] = (prod[3, m] + across[m]).astype(jnp.bfloat16)
+        ig[m] = (prod[1, m] + across[m]).astype(jnp.bfloat16)
         return carry
 
     lax.fori_loop(0, cols, column, 0)
     store = pltpu.make_async_copy(ig, ig_hbm, load_sem.at[0])
     store.start()
+    for mine, edges, _ in inputs:
+        mine.wait_send()
+        for copy in edges:
+            copy.wait_send()
 
     def end(e, carry):
         do_end(e)
@@ -387,7 +389,7 @@
         in_specs=[anywhere] * 3,
         out_specs=(anywhere, anywhere),
         scratch_shapes=[
-            pltpu.VMEM((126, out_rows, lats), bf16),
+            pltpu.VMEM((180, out_rows, lats), bf16),
             pltpu.VMEM((depth, cells), bf16),
             pltpu.VMEM((4, cols, in_rows, lats), bf16),
             pltpu.VMEM((2 * in_rows, cells), bf16),
@@ -404,8 +406,8 @@
             pltpu.VMEM((cols, in_rows, lats), f32),
             pltpu.VMEM((cols, in_rows, lats), bf16),
             pltpu.SemaphoreType.DMA((5 + 2 * CHUNKS,)),
-            pltpu.SemaphoreType.DMA((6,)),
-            pltpu.SemaphoreType.DMA((6,)),
+            pltpu.SemaphoreType.DMA((9,)),
+            pltpu.SemaphoreType.DMA((9,)),
             pltpu.SemaphoreType.DMA((3,)),
             pltpu.SemaphoreType.DMA((3,)),
             pltpu.SemaphoreType.DMA((CHUNKS, 26)),

time: 185 us -> 154 us (0.83); the launches traced: 182 us -> 154 us
  Pallas kernels: 172 us -> 144 us
    pallas_call x1, Pallas kernels: 172 us -> 144 us  [local(): pl.pallas_call(functools.partial(backward_kernel, scale), out_shape=(jax....]
where the time goes in v3:
time: 154 us
  Pallas kernels  144 us (94%)
  local copies, waits for them, and re-layouts  9.68 us (6%)
    pallas_call x1, Pallas kernels, local(): pl.pallas_call(functools.partial(backward_kernel, scale), out_shape=(jax....  144 us
    unnamed x2, local copies, waits for them, and re-layouts  9.68 us

profile of v3, /device:TPU:0, one launch (start us, length us, event | category | flops | bytes accessed | tf_op | source)
XLA Modules:
  0.0 154.0 jit_solution(17573460195510410361)
XLA Ops:
  0.6 143.6 %backward.1 = (bf16[18,256,128]{2,1,0:T(8,128)(2,1)}, f32[1728,1024]{1,0:T(8,128)}) custom-call(bf16[18,256,128]{2,1,0:T(8,128)(2,1)} %bitcast.14, bf16[3,18,64,128]{3,2,1,0:T(8,128)(2,1)} %bitcast.15, bf16[1728,1024]{1,0:T(8,128)(2,1)} %bitcast.12), custom_call_target="tpu_custom_call" | custom-call | tf_op jit(solution)/shard_map/backward/pallas_call | solution.py:383
  144.3 2.4 %copy.7 = bf16[256,1,18,128]{3,0,2,1:T(8,128)(2,1)} copy(bf16[256,1,18,128]{3,0,2,1:T(8,128)(2,1)} %bitcast.13) | data formatting | bytes 2359296
  146.7 7.3 %copy.8 = f32[3,3,3,64,1024]{4,3,2,1,0:T(8,128)} copy(f32[3,3,3,64,1024]{4,3,2,1,0:T(8,128)} %bitcast.11) | data formatting | bytes 14155776

commit v4 on v3

v4 whole, which is shorter than its diff:
```python
import functools
import math

import jax
import jax.numpy as jnp
from jax import lax
from jax.experimental import pallas as pl
from jax.experimental.pallas import tpu as pltpu
from jax.sharding import PartitionSpec as P

DILATIONS = (6, 12, 18)
BASES = (0, 48, 108)
MESH = pl.DeviceIdType.MESH
Y, Z, X = 4, 4, 2
CHUNKS = 6
LAG = (1, 2, 3, 4, 5, 6)
GROUPS = 3


def mod4(v):
    return lax.rem(v, 4)


def aligned(v, m, size):
    return pl.ds(pl.multiple_of(v, m), size)


def backward_kernel(
    scale, feat_hbm, cot_hbm, w_hbm, ig_hbm, kg_hbm,
    ext, stack, raw, flat, wcol, wt, part, first, second, low, third, prod, other, across, ig,
    load_sem, halo_send, halo_recv, feat_send, feat_recv, sum_send, sum_recv, ig_send, ig_recv,
):
    lon = lax.axis_index("lon")
    ch = lax.axis_index("ch")
    lons = Y * Z * X
    y, z, x = lon // (Z * X), lax.rem(lon // X, Z), lax.rem(lon, X)
    xh, core = ch // 2, lax.rem(ch, 2)
    cols = feat_hbm.shape[0]
    in_rows = feat_hbm.shape[1]
    out_rows = cot_hbm.shape[2]
    taps = 9 * out_rows
    rows = taps // 4
    here = (y, z)

    def at(dy, dz, dx):
        return (mod4(y + dy) * (Z * X) + mod4(z + dz) * X + lax.rem(x + dx, X), ch)

    hops = [(d, 0, 0) for d in (1, 2, 3)], [(0, d, 0) for d in (1, 2, 3)]
    twin = at(0, 0, 1)
    pair = lon - x
    mate = (lon, xh * 2 + 1 - core)
    far = (pair + 1 - x, (1 - xh) * 2 + core)
    outer = [(lax.rem(pair + step, lons), ch) for step in (lons - 2, lons - 1, 2, 3)]
    halo_to = [(lax.rem(pair + lons - 2 + 4 * x + i, lons), ch) for i in range(2)]

    def load_w(chip, who):
        columns = aligned((chip * 2 + who) * in_rows, 128, in_rows)
        return pltpu.make_async_copy(w_hbm.at[:, columns], wcol.at[pl.ds(0, 3 * taps)], load_sem.at[0])

    load_f = pltpu.make_async_copy(feat_hbm, raw.at[core], load_sem.at[1])
    loads = [
        pltpu.make_async_copy(cot_hbm.at[k], ext.at[pl.ds(BASES[k] + d + x * cols, cols)], load_sem.at[2 + k])
        for k, d in enumerate(DILATIONS)
    ]
    for copy in loads:
        copy.start()
    load_f.start()
    load_w(1 - xh, 1 - core).start()

    barrier = pltpu.get_barrier_semaphore()
    peers = [at(*hop) for hop in hops[0] + hops[1]] + [twin, mate, far] + outer
    for peer in peers:
        pl.semaphore_signal(barrier, inc=1, device_id=peer, device_id_type=MESH)
    pl.semaphore_wait(barrier, len(peers))

    def remote(src, dst, send, recv, peer):
        return pltpu.make_async_remote_copy(
            src_ref=src, dst_ref=dst, send_sem=send, recv_sem=recv, device_id=peer, device_id_type=MESH
        )

    inputs = []
    for k, d in enumerate(DILATIONS):
        base = BASES[k]
        mine = remote(
            cot_hbm.at[k], ext.at[pl.ds(base + d + x * cols, cols)], halo_send.at[3 * k], halo_recv.at[3 * k], twin
        )
        edges = [
            remote(
                cot_hbm.at[k, pl.ds(x * (cols - d), d)],
                ext.at[pl.ds(base + (1 - x) * (2 * cols + d), d)],
                halo_send.at[3 * k + 1 + i],
                halo_recv.at[3 * k + 1 + (1 - x)],
                halo_to[i],
            )
            for i in range(2)
        ]
        for copy in edges + [mine]:
            copy.start()
        before = ext.at[pl.ds(base, d)]
        after = ext.at[pl.ds(base + 2 * cols + d, d)]
        arrivals = [
            remote(before, before, halo_send.at[3 * k + 1], halo_recv.at[3 * k + 1], halo_to[0]),
            remote(after, after, halo_send.at[3 * k + 1], halo_recv.at[3 * k + 2], halo_to[0]),
        ]
        inputs.append((mine, edges, arrivals))
    feat_mate = remote(feat_hbm, raw.at[core], feat_send.at[0], feat_recv.at[0], mate)
    feat_far = remote(feat_hbm, raw.at[2 + core], feat_send.at[1], feat_recv.at[1], far)
    feat_on = remote(raw.at[2 + core], raw.at[2 + core], feat_send.at[2], feat_recv.at[2], mate)
    feat_mate.start()
    feat_far.start()

    lane = lax.broadcasted_iota(jnp.int32, (out_rows, 128), 1)

    def build(k, side, slot):
        d, base = DILATIONS[k], BASES[k]

        def column(m, carry):
            for lon_tap in range(3):
                v = ext[base + d + side * cols + m - d * (lon_tap - 1)].astype(jnp.float32)
                for lat_tap in range(3):
                    if lat_tap == 0:
                        moved = jnp.where(lane < 128 - d, pltpu.roll(v, 128 - d, 1), 0.0)
                    elif lat_tap == 1:
                        moved = v
                    else:
                        moved = jnp.where(lane >= d, pltpu.roll(v, d, 1), 0.0)
                    row = slot * taps + (lat_tap * 3 + lon_tap) * out_rows
                    stack[pl.ds(row, out_rows), aligned(m * 128, 128, 128)] = moved.astype(jnp.bfloat16)
            return carry

        lax.fori_loop(0, cols, column, 0)

    def flatten(chip):
        def column(m, carry):
            for jj in range(2):
                flat[pl.ds(jj * in_rows, in_rows), aligned(m * 128, 128, 128)] = raw[chip * 2 + jj, m]
            return carry

        lax.fori_loop(0, cols, column, 0)

    def order(e):
        far_side = (e >= 2) & (e < 5)
        return far_side, jnp.where(e < 2, e, jnp.where(far_side, e - 2, 2))

    def tile(h, block, sub, e):
        return part.at[e, aligned(mod4(here[h] + block) * rows, 8, rows), pl.ds(h * 256 + sub * 128, 128)]

    def rs1(e, h):
        up, down = at(*hops[h][0]), at(*hops[h][2])

        def send(i, src, peer):
            return remote(src, first.at[e, h, i], sum_send.at[e, h * 6 + i], sum_recv.at[e, h * 6 + i], peer)

        through = [send(0, tile(h, 2, 0, e), up), send(1, tile(h, 2, 1, e), down)]
        alone = [send(2, tile(h, 1, 1, e), up), send(3, tile(h, 3, 0, e), down)]
        both = [send(4, tile(h, 1, 0, e), up), send(5, tile(h, 3, 1, e), down)]
        return through, alone, both

    def piece(h, q, base_row=0, base_col=0):
        return (
            aligned(base_row + here[h] * rows + (q // 2) * (rows // 2), 8, rows // 2),
            aligned(base_col + h * 256 + lax.rem(q, 2) * 128, 128, 128),
        )

    def rs2(e, h):
        out = []
        for d in range(3):
            q = mod4(here[1 - h] + d + 1)
            slot = 12 + h * 3 + d
            r, c = piece(h, q)
            out.append(
                remote(part.at[e, r, c], second.at[e, h, d], sum_send.at[e, slot], sum_recv.at[e, slot], at(*hops[1 - h][d]))
            )
        return out

    def swap(e, h):
        return remote(low.at[e, h], third.at[e, h], sum_send.at[e, 18 + h], sum_recv.at[e, 18 + h], at(0, 0, 1))

    def corner(e):
        far_side, k = order(e)
        return k * taps, jnp.where(far_side, 1 - xh, xh) * 512

    def ag2_local(e, h):
        r, c = piece(h, here[1 - h], *corner(e))
        return pltpu.make_async_copy(low.at[e, h], kg_hbm.at[r, c], load_sem.at[5 + 2 * e + h])

    def ag2(e, h):
        r, c = piece(h, here[1 - h], *corner(e))
        return [
            remote(
                low.at[e, h], kg_hbm.at[r, c], sum_send.at[e, 20 + h * 3 + d], sum_recv.at[e, 20 + h * 3 + d], at(*hops[1 - h][d])
            )
            for d in range(3)
        ]

    def ag1(e, h):
        base_row, base_col = corner(e)
        up, down = at(*hops[h][0]), at(*hops[h][2])

        def send(i, block, sub, width, peer):
            area = kg_hbm.at[
                aligned(base_row + mod4(here[h] + block) * rows, 8, rows),
                aligned(base_col + h * 256 + sub * 128, 128, width),
            ]
            return remote(area, area, sum_send.at[e, 26 + h * 4 + i], sum_recv.at[e, 26 + h * 4 + i], peer)

        near = [send(0, 0, 0, 256, up), send(1, 0, 0, 256, down)]
        onward = [send(2, 3, 0, 128, up), send(3, 1, 1, 128, down)]
        return near, onward

    def do_chunk(e):
        far_side, k = order(e)
        slot = jnp.where(far_side, k, 3)
        for h in range(2):
            part[e, :, pl.ds(h * 256, 256)] = lax.dot_general(
                stack[aligned(slot * taps, 16, taps), :],
                flat[pl.ds(h * 256, 256), :],
                (((1,), (1,)), ((), ())),
                preferred_element_type=jnp.float32,
            )
            through, alone, _ = rs1(e, h)
            for copy in through + alone:
                copy.start()

    def do_rs1(e):
        for h in range(2):
            through, _, both = rs1(e, h)
            for i in range(2):
                through[i].wait()
                block, cols_at = (1, 3)[i], pl.ds(h * 256 + i * 128, 128)

                def step(n, carry):
                    r = aligned(mod4(here[h] + block) * rows + n * 16, 8, 16)
                    part[e, r, cols_at] = part[e, r, cols_at] + first[e, h, i, aligned(n * 16, 16, 16), :]
                    return carry

                lax.fori_loop(0, rows // 16, step, 0)
                both[i].start()

    def do_rs2(e):
        for h in range(2):
            _, alone, both = rs1(e, h)
            for copy in alone + both:
                copy.wait()

            def step(n, carry):
                r = aligned(n * 16, 16, 16)
                mine = aligned(here[h] * rows + n * 16, 8, 16)
                for sub, (a, b) in enumerate(((3, 4), (2, 5))):
                    c = pl.ds(h * 256 + sub * 128, 128)
                    part[e, mine, c] = part[e, mine, c] + (first[e, h, a, r, :] + first[e, h, b, r, :])
                return carry

            lax.fori_loop(0, rows // 16, step, 0)
            for copy in rs2(e, h):
                copy.start()

    def do_swap(e):
        for h in range(2):
            for copy in rs2(e, h):
                copy.wait()
            r, c = piece(h, here[1 - h])
            low[e, h] = (part[e, r, c] + second[e, h, 0]) + (second[e, h, 1] + second[e, h, 2])
            swap(e, h).start()

    def do_ag2(e):
        for h in range(2):
            swap(e, h).wait()
            low[e, h] = (low[e, h] + third[e, h]) * scale
            ag2_local(e, h).start()
            for copy in ag2(e, h):
                copy.start()

    def do_ag1(e):
        for h in range(2):
            ag2_local(e, h).wait()
            for copy in ag2(e, h):
                copy.wait()
            for copy in ag1(e, h)[0]:
                copy.start()

    def do_onward(e):
        for h in range(2):
            near, onward = ag1(e, h)
            near[1].wait_send()
            near[0].wait()
            onward[0].start()
            near[1].wait_recv()
            onward[1].start()

    def do_end(e):
        for h in range(2):
            for copy in ag1(e, h)[1]:
                copy.wait()

    wide = cols // GROUPS

    def turn(slot):
        wt[slot] = wcol[...].T

    def ig_group(slot, dst, q):
        def tile_of(i, carry):
            m = q * (wide // 2) + i
            res = jnp.dot(
                wt[slot], stack[pl.ds(0, wt.shape[2]), aligned(m * 256, 256, 256)], preferred_element_type=jnp.float32
            )
            prod[dst, 2 * m] = res[:, :128]
            prod[dst, 2 * m + 1] = res[:, 128:]
            return carry

        lax.fori_loop(0, wide // 2, tile_of, 0)

    def ig_mate(part_of, q):
        group = pl.ds(q * wide, wide)
        slot = part_of * GROUPS + q
        return remote(prod.at[0, group], other.at[part_of, group], ig_send.at[slot], ig_recv.at[slot], mate)

    def ig_far(q):
        group = pl.ds(q * wide, wide)
        slot = 2 * GROUPS + q
        return remote(prod.at[1, group], across.at[group], ig_send.at[slot], ig_recv.at[slot], far)

    def finish_far(q):
        ig_mate(1, q).wait()

        def column(i, carry):
            m = q * wide + i
            prod[1, m] = prod[1, m] + other[1, m]
            return carry

        lax.fori_loop(0, wide, column, 0)
        ig_far(q).start()

    def far_group(q, carry):
        ig_group(0, 0, q)
        ig_mate(1, q).start()
        ig_group(1, 1, q)

        @pl.when(q > 0)
        def _():
            finish_far(q - 1)

        return carry

    pad = wcol.shape[0] - 3 * taps
    wcol[pl.ds(3 * taps, pad), :] = jnp.zeros((pad, wcol.shape[1]), wcol.dtype)
    load_w(1 - xh, 1 - core).wait()
    turn(0)
    load_w(1 - xh, core).start()
    load_w(1 - xh, core).wait()
    turn(1)
    load_w(xh, 1 - core).start()

    def arrived(k):
        mine, edges, arrivals = inputs[k]
        loads[k].wait()
        mine.wait_recv()
        for copy in arrivals:
            copy.wait_recv()

    def body(s, carry):
        @pl.when(s == 0)
        def _():
            load_f.wait()
            feat_mate.wait()
            flatten(0)
            arrived(0)
            build(0, x, 3)

        @pl.when(s == 1)
        def _():
            arrived(1)
            build(1, x, 3)

        @pl.when(s == 2)
        def _():
            feat_far.wait()
            feat_on.start()
            build(0, 1 - x, 0)
            feat_on.wait()
            flatten(1)

        @pl.when(s == 3)
        def _():
            build(1, 1 - x, 1)

        @pl.when(s == 4)
        def _():
            arrived(2)
            build(2, 1 - x, 2)

        @pl.when(s == 5)
        def _():
            flatten(0)
            build(2, x, 3)

        @pl.when(s < CHUNKS)
        def _():
            do_chunk(s)

        @pl.when(s == 4)
        def _():
            lax.fori_loop(0, GROUPS, far_group, 0)
            finish_far(GROUPS - 1)

        @pl.when(s == 6)
        def _():
            load_w(xh, 1 - core).wait()
            turn(0)
            load_w(xh, core).start()
            for k in range(3):
                build(k, x, k)
            load_w(xh, core).wait()
            turn(1)

        @pl.when((s >= 7) & (s < 7 + GROUPS))
        def _():
            q = s - 7
            ig_group(0, 0, q)
            ig_mate(0, q).start()
            ig_group(1, 2, q)

        for lag, work in zip(LAG[::-1], (do_onward, do_ag1, do_ag2, do_swap, do_rs2, do_rs1)):

            @pl.when((s >= lag) & (s < CHUNKS + lag))
            def _():
                work(s - lag)

        return carry

    lax.fori_loop(0, CHUNKS + LAG[-1], body, 0)

    def last(q, carry):
        ig_mate(0, q).wait()
        ig_far(q).wait()

        def column(i, inner):
            m = q * wide + i
            ig[m] = (prod[2, m] + other[0, m] + across[m]).astype(jnp.bfloat16)
            return inner

        lax.fori_loop(0, wide, column, 0)
        return carry

    lax.fori_loop(0, GROUPS, last, 0)
    store = pltpu.make_async_copy(ig, ig_hbm, load_sem.at[0])
    store.start()
    for mine, edges, _ in inputs:
        mine.wait_send()
        for copy in edges:
            copy.wait_send()

    def end(e, carry):
        do_end(e)
        return carry

    lax.fori_loop(0, CHUNKS, end, 0)
    store.wait()


def local(features, cotangent, weights):
    in_rows, _, cols, lats = features.shape
    out_rows, in_total = weights.shape[3:]
    cells = cols * lats
    taps = 9 * out_rows
    rows = taps // 4
    depth = -(-3 * taps // 256) * 256
    scale = 1.0 / math.sqrt(cells * lax.axis_size("lon"))
    f32, bf16 = jnp.float32, jnp.bfloat16
    anywhere = pl.BlockSpec(memory_space=pl.ANY)
    ig, kg = pl.pallas_call(
        functools.partial(backward_kernel, scale),
        out_shape=(
            jax.ShapeDtypeStruct((cols, in_rows, lats), bf16),
            jax.ShapeDtypeStruct((3 * taps, in_total), f32),
        ),
        in_specs=[anywhere] * 3,
        out_specs=(anywhere, anywhere),
        scratch_shapes=[
            pltpu.VMEM((180, out_rows, lats), bf16),
            pltpu.VMEM((4 * taps, cells), bf16),
            pltpu.VMEM((4, cols, in_rows, lats), bf16),
            pltpu.VMEM((2 * in_rows, cells), bf16),
            pltpu.VMEM((depth, in_rows), bf16),
            pltpu.VMEM((2, in_rows, depth), bf16),
            pltpu.VMEM((CHUNKS, taps, 512), f32),
            pltpu.VMEM((CHUNKS, 2, 6, rows, 128), f32),
            pltpu.VMEM((CHUNKS, 2, 3, rows // 2, 128), f32),
            pltpu.VMEM((CHUNKS, 2, rows // 2, 128), f32),
            pltpu.VMEM((CHUNKS, 2, rows // 2, 128), f32),
            pltpu.VMEM((3, cols, in_rows, lats), f32),
            pltpu.VMEM((2, cols, in_rows, lats), f32),
            pltpu.VMEM((cols, in_rows, lats), f32),
            pltpu.VMEM((cols, in_rows, lats), bf16),
            pltpu.SemaphoreType.DMA((5 + 2 * CHUNKS,)),
            pltpu.SemaphoreType.DMA((9,)),
            pltpu.SemaphoreType.DMA((9,)),
            pltpu.SemaphoreType.DMA((3,)),
            pltpu.SemaphoreType.DMA((3,)),
            pltpu.SemaphoreType.DMA((CHUNKS, 34)),
            pltpu.SemaphoreType.DMA((CHUNKS, 34)),
            pltpu.SemaphoreType.DMA((3 * GROUPS,)),
            pltpu.SemaphoreType.DMA((3 * GROUPS,)),
        ],
        compiler_params=pltpu.CompilerParams(
            collective_id=1, has_side_effects=True, vmem_limit_bytes=52 * 1024 * 1024
        ),
        name="backward",
    )(
        features.reshape(in_rows, cols, lats).transpose(1, 0, 2),
        cotangent.reshape(3, out_rows, cols, lats).transpose(0, 2, 1, 3),
        weights.reshape(3 * taps, in_total),
    )
    input_grad = ig.transpose(1, 0, 2).reshape(in_rows, 1, cols, lats)
    return (input_grad, kg.reshape(3, 3, 3, out_rows, in_total))


def solution(mesh):
    return jax.shard_map(
        local,
        mesh=mesh,
        in_specs=(
            P("ch", None, "lon", None),
            P(None, "ch", None, "lon", None),
            P(None, None, None, "ch", None),
        ),
        out_specs=(P("ch", None, "lon", None), P(None, None, None, "ch", None)),
        check_vma=False,
    )
```

time: 154 us -> 143 us (0.929)
  Pallas kernels: 144 us -> 131 us
    pallas_call x1, Pallas kernels: 144 us -> 131 us  [local(): pl.pallas_call(functools.partial(backward_kernel, scale), out_shape=(jax....]
    unnamed x2 -> x4, local copies, waits for them, and re-layouts: 9.68 us -> 10.8 us
where the time goes in v4:
time: 143 us; the launch traced here: 142 us
  Pallas kernels  131 us (92%)
  local copies, waits for them, and re-layouts  10.8 us (8%)
    pallas_call x1, Pallas kernels, local(): pl.pallas_call(functools.partial(backward_kernel, scale), out_shape=(jax....  131 us
    unnamed x4, local copies, waits for them, and re-layouts  10.8 us

profile of v4, /device:TPU:0, one launch (start us, length us, event | category | flops | bytes accessed | tf_op | source)
XLA Modules:
  0.0 142.3 jit_solution(7098124703084878334)
XLA Ops:
  0.6 0.0 copy-start
  0.6 1.2 copy-done
  1.8 130.8 %backward.1 = (bf16[18,256,128]{2,1,0:T(8,128)(2,1)}, f32[1728,1024]{1,0:T(8,128)}) custom-call(bf16[18,256,128]{2,1,0:T(8,128)(2,1)} %bitcast.15, bf16[3,18,64,128]{3,2,1,0:T(8,128)(2,1)S(1)} %bitcast.11, bf16[1728,1024]{1,0:T(8,128)(2,1)} %bitcast.13), custom_call_target="tpu_custom_call" | custom-call | tf_op jit(solution)/shard_map/backward/pallas_call | solution.py:471
  132.6 2.4 %copy.7 = bf16[256,1,18,128]{3,0,2,1:T(8,128)(2,1)} copy(bf16[256,1,18,128]{3,0,2,1:T(8,128)(2,1)} %bitcast.14) | data formatting | bytes 2359296
  135.0 7.3 %copy.8 = f32[3,3,3,64,1024]{4,3,2,1,0:T(8,128)} copy(f32[3,3,3,64,1024]{4,3,2,1,0:T(8,128)} %bitcast.12) | data formatting | bytes 14155776
Async XLA Ops:
  0.6 1.2 copy-start

commit v5 on v4

--- a/solution.py
+++ b/solution.py
@@ -94,8 +94,6 @@
             )
             for i in range(2)
         ]
-        for copy in edges + [mine]:
-            copy.start()
         before = ext.at[pl.ds(base, d)]
         after = ext.at[pl.ds(base + 2 * cols + d, d)]
         arrivals = [
@@ -103,6 +101,12 @@
             remote(after, after, halo_send.at[3 * k + 1], halo_recv.at[3 * k + 2], halo_to[0]),
         ]
         inputs.append((mine, edges, arrivals))
+    def send_branch(k):
+        mine, edges, _ = inputs[k]
+        for copy in edges + [mine]:
+            copy.start()
+
+    send_branch(0)
     feat_mate = remote(feat_hbm, raw.at[core], feat_send.at[0], feat_recv.at[0], mate)
     feat_far = remote(feat_hbm, raw.at[2 + core], feat_send.at[1], feat_recv.at[1], far)
     feat_on = remote(raw.at[2 + core], raw.at[2 + core], feat_send.at[2], feat_recv.at[2], mate)
@@ -331,7 +335,7 @@
         lax.fori_loop(0, wide, column, 0)
         ig_far(q).start()
 
-    def far_group(q, carry):
+    def far_group(q):
         ig_group(0, 0, q)
         ig_mate(1, q).start()
         ig_group(1, 1, q)
@@ -339,14 +343,13 @@
         @pl.when(q > 0)
         def _():
             finish_far(q - 1)
-
-        return carry
 
     pad = wcol.shape[0] - 3 * taps
     wcol[pl.ds(3 * taps, pad), :] = jnp.zeros((pad, wcol.shape[1]), wcol.dtype)
     load_w(1 - xh, 1 - core).wait()
     turn(0)
     load_w(1 - xh, core).start()
+    send_branch(1)
     load_w(1 - xh, core).wait()
     turn(1)
     load_w(xh, 1 - core).start()
@@ -358,6 +361,14 @@
         for copy in arrivals:
             copy.wait_recv()
 
+    def at_tick(u, work):
+        early = (u == 0) | (u == 2)
+        late = (u >= 4) & (u < 4 + CHUNKS - 2)
+
+        @pl.when(early | late)
+        def _():
+            work(jnp.where(u < 4, lax.div(u, 2), u - 2))
+
     def body(s, carry):
         @pl.when(s == 0)
         def _():
@@ -367,12 +378,12 @@
             arrived(0)
             build(0, x, 3)
 
-        @pl.when(s == 1)
+        @pl.when(s == 2)
         def _():
             arrived(1)
             build(1, x, 3)
 
-        @pl.when(s == 2)
+        @pl.when(s == 4)
         def _():
             feat_far.wait()
             feat_on.start()
@@ -380,31 +391,33 @@
             feat_on.wait()
             flatten(1)
 
-        @pl.when(s == 3)
+        @pl.when(s == 5)
         def _():
             build(1, 1 - x, 1)
 
-        @pl.when(s == 4)
+        @pl.when(s == 6)
         def _():
             arrived(2)
             build(2, 1 - x, 2)
 
-        @pl.when(s == 5)
+        @pl.when(s == 7)
         def _():
             flatten(0)
             build(2, x, 3)
 
-        @pl.when(s < CHUNKS)
-        def _():
-            do_chunk(s)
-
-        @pl.when(s == 4)
-        def _():
-            lax.fori_loop(0, GROUPS, far_group, 0)
+        at_tick(s, do_chunk)
+
+        @pl.when(s == 0)
+        def _():
+            send_branch(2)
+
+        @pl.when((s >= 7) & (s < 7 + GROUPS))
+        def _():
+            far_group(s - 7)
+
+        @pl.when(s == 7 + GROUPS)
+        def _():
             finish_far(GROUPS - 1)
-
-        @pl.when(s == 6)
-        def _():
             load_w(xh, 1 - core).wait()
             turn(0)
             load_w(xh, core).start()
@@ -413,22 +426,19 @@
             load_w(xh, core).wait()
             turn(1)
 
-        @pl.when((s >= 7) & (s < 7 + GROUPS))
-        def _():
-            q = s - 7
+        @pl.when((s >= 8 + GROUPS) & (s < 8 + 2 * GROUPS))
+        def _():
+            q = s - 8 - GROUPS
             ig_group(0, 0, q)
             ig_mate(0, q).start()
             ig_group(1, 2, q)
 
         for lag, work in zip(LAG[::-1], (do_onward, do_ag1, do_ag2, do_swap, do_rs2, do_rs1)):
-
-            @pl.when((s >= lag) & (s < CHUNKS + lag))
-            def _():
-                work(s - lag)
+            at_tick(s - lag, work)
 
         return carry
 
-    lax.fori_loop(0, CHUNKS + LAG[-1], body, 0)
+    lax.fori_loop(0, 8 + LAG[-1], body, 0)
 
     def last(q, carry):
         ig_mate(0, q).wait()

time: 143 us -> 150 us (1.049)
  Pallas kernels: 131 us -> 138 us
    pallas_call x1, Pallas kernels: 131 us -> 138 us  [local(): pl.pallas_call(functools.partial(backward_kernel, scale), out_shape=(jax....]
where the time goes in v5:
time: 150 us
  Pallas kernels  138 us (92%)
  local copies, waits for them, and re-layouts  10.8 us (7%)
    pallas_call x1, Pallas kernels, local(): pl.pallas_call(functools.partial(backward_kernel, scale), out_shape=(jax....  138 us
    unnamed x4, local copies, waits for them, and re-layouts  10.8 us

profile of v5, /device:TPU:0, one launch (start us, length us, event | category | flops | bytes accessed | tf_op | source)
XLA Modules:
  0.0 149.9 jit_solution(14368782879431757085)
XLA Ops:
  0.6 0.0 copy-start
  0.6 1.2 copy-done
  1.8 138.4 %backward.1 = (bf16[18,256,128]{2,1,0:T(8,128)(2,1)}, f32[1728,1024]{1,0:T(8,128)}) custom-call(bf16[18,256,128]{2,1,0:T(8,128)(2,1)} %bitcast.15, bf16[3,18,64,128]{3,2,1,0:T(8,128)(2,1)S(1)} %bitcast.11, bf16[1728,1024]{1,0:T(8,128)(2,1)} %bitcast.13), custom_call_target="tpu_custom_call" | custom-call | tf_op jit(solution)/shard_map/backward/pallas_call | solution.py:481
  140.2 2.4 %copy.7 = bf16[256,1,18,128]{3,0,2,1:T(8,128)(2,1)} copy(bf16[256,1,18,128]{3,0,2,1:T(8,128)(2,1)} %bitcast.14) | data formatting | bytes 2359296
  142.6 7.3 %copy.8 = f32[3,3,3,64,1024]{4,3,2,1,0:T(8,128)} copy(f32[3,3,3,64,1024]{4,3,2,1,0:T(8,128)} %bitcast.12) | data formatting | bytes 14155776
Async XLA Ops:
  0.6 1.2 copy-start

commit v6 on v4

--- a/solution.py
+++ b/solution.py
@@ -331,7 +331,7 @@
         lax.fori_loop(0, wide, column, 0)
         ig_far(q).start()
 
-    def far_group(q, carry):
+    def far_group(q):
         ig_group(0, 0, q)
         ig_mate(1, q).start()
         ig_group(1, 1, q)
@@ -339,8 +339,6 @@
         @pl.when(q > 0)
         def _():
             finish_far(q - 1)
-
-        return carry
 
     pad = wcol.shape[0] - 3 * taps
     wcol[pl.ds(3 * taps, pad), :] = jnp.zeros((pad, wcol.shape[1]), wcol.dtype)
@@ -398,12 +396,15 @@
         def _():
             do_chunk(s)
 
-        @pl.when(s == 4)
-        def _():
-            lax.fori_loop(0, GROUPS, far_group, 0)
+        @pl.when((s >= 5) & (s < 5 + GROUPS))
+        def _():
+            far_group(s - 5)
+
+        @pl.when(s == 5 + GROUPS)
+        def _():
             finish_far(GROUPS - 1)
 
-        @pl.when(s == 6)
+        @pl.when(s == 8)
         def _():
             load_w(xh, 1 - core).wait()
             turn(0)
@@ -413,14 +414,14 @@
             load_w(xh, core).wait()
             turn(1)
 
-        @pl.when((s >= 7) & (s < 7 + GROUPS))
-        def _():
-            q = s - 7
+        @pl.when((s >= 9) & (s < 9 + GROUPS))
+        def _():
+            q = s - 9
             ig_group(0, 0, q)
             ig_mate(0, q).start()
             ig_group(1, 2, q)
 
-        for lag, work in zip(LAG[::-1], (do_onward, do_ag1, do_ag2, do_swap, do_rs2, do_rs1)):
+        for lag, work in zip(LAG, (do_rs1, do_rs2, do_swap, do_ag2, do_ag1, do_onward)):
 
             @pl.when((s >= lag) & (s < CHUNKS + lag))
             def _():
@@ -471,8 +472,8 @@
     ig, kg = pl.pallas_call(
         functools.partial(backward_kernel, scale),
         out_shape=(
-            jax.ShapeDtypeStruct((cols, in_rows, lats), bf16),
-            jax.ShapeDtypeStruct((3 * taps, in_total), f32),
+            pltpu.VMEM((cols, in_rows, lats), bf16),
+            pltpu.VMEM((3 * taps, in_total), f32),
         ),
         in_specs=[anywhere] * 3,
         out_specs=(anywhere, anywhere),

time: 143 us -> 130 us (0.909)
  local copies, waits for them, and re-layouts: 10.8 us -> 3.98 us
  Pallas kernels: 131 us -> 125 us
    unnamed x4 -> x2, local copies, waits for them, and re-layouts: 10.8 us -> 3.98 us
    pallas_call x1, Pallas kernels: 131 us -> 125 us  [local(): pl.pallas_call(functools.partial(backward_kernel, scale), out_shape=(pltp...]
where the time goes in v6:
time: 130 us
  Pallas kernels  125 us (96%)
  local copies, waits for them, and re-layouts  3.98 us (3%)
    pallas_call x1, Pallas kernels, local(): pl.pallas_call(functools.partial(backward_kernel, scale), out_shape=(pltp...  125 us
    unnamed x2, local copies, waits for them, and re-layouts  3.98 us

profile of v6, /device:TPU:0, one launch (start us, length us, event | category | flops | bytes accessed | tf_op | source)
XLA Modules:
  0.0 129.7 jit_solution(12954016138920716023)
XLA Ops:
  0.6 125.1 %backward.1 = (bf16[18,256,128]{2,1,0:T(8,128)(2,1)S(1)}, f32[1728,1024]{1,0:T(8,128)S(1)}) custom-call(bf16[18,256,128]{2,1,0:T(8,128)(2,1)} %bitcast.14, bf16[3,18,64,128]{3,2,1,0:T(8,128)(2,1)} %bitcast.15, bf16[1728,1024]{1,0:T(8,128)(2,1)} %bitcast.13), custom_call_target="tpu_custom_call" | custom-call | tf_op jit(solution)/shard_map/backward/pallas_call | solution.py:472
  125.7 1.0 copy.7
  126.7 3.0 %copy.8 = f32[3,3,3,64,1024]{4,3,2,1,0:T(8,128)} copy(f32[3,3,3,64,1024]{4,3,2,1,0:T(8,128)S(1)} %bitcast.11) | data formatting | bytes 14155776

commit v7 on v6

--- a/solution.py
+++ b/solution.py
@@ -81,8 +81,13 @@
     inputs = []
     for k, d in enumerate(DILATIONS):
         base = BASES[k]
+        start = (1 - x) * (cols - d)
         mine = remote(
-            cot_hbm.at[k], ext.at[pl.ds(base + d + x * cols, cols)], halo_send.at[3 * k], halo_recv.at[3 * k], twin
+            cot_hbm.at[k, pl.ds(start, d)],
+            ext.at[pl.ds(base + d + x * cols + start, d)],
+            halo_send.at[3 * k],
+            halo_recv.at[3 * k],
+            twin,
         )
         edges = [
             remote(
@@ -103,6 +108,18 @@
             remote(after, after, halo_send.at[3 * k + 1], halo_recv.at[3 * k + 2], halo_to[0]),
         ]
         inputs.append((mine, edges, arrivals))
+    rests = []
+    for k, d in enumerate(DILATIONS[:2]):
+        rests.append(
+            remote(
+                cot_hbm.at[k, pl.ds(x * d, cols - d)],
+                ext.at[pl.ds(BASES[k] + d + x * cols + x * d, cols - d)],
+                halo_send.at[9 + k],
+                halo_recv.at[9 + k],
+                twin,
+            )
+        )
+        rests[k].start()
     feat_mate = remote(feat_hbm, raw.at[core], feat_send.at[0], feat_recv.at[0], mate)
     feat_far = remote(feat_hbm, raw.at[2 + core], feat_send.at[1], feat_recv.at[1], far)
     feat_on = remote(raw.at[2 + core], raw.at[2 + core], feat_send.at[2], feat_recv.at[2], mate)
@@ -139,8 +156,7 @@
         lax.fori_loop(0, cols, column, 0)
 
     def order(e):
-        far_side = (e >= 2) & (e < 5)
-        return far_side, jnp.where(e < 2, e, jnp.where(far_side, e - 2, 2))
+        return e >= 3, lax.rem(e, 3)
 
     def tile(h, block, sub, e):
         return part.at[e, aligned(mod4(here[h] + block) * rows, 8, rows), pl.ds(h * 256 + sub * 128, 128)]
@@ -367,30 +383,32 @@
 
         @pl.when(s == 1)
         def _():
+            do_rs1(0)
             arrived(1)
             build(1, x, 3)
 
         @pl.when(s == 2)
         def _():
+            arrived(2)
+            build(2, x, 3)
+
+        @pl.when(s == 3)
+        def _():
             feat_far.wait()
             feat_on.start()
+            rests[0].wait()
             build(0, 1 - x, 0)
             feat_on.wait()
             flatten(1)
 
-        @pl.when(s == 3)
-        def _():
+        @pl.when(s == 4)
+        def _():
+            rests[1].wait()
             build(1, 1 - x, 1)
 
-        @pl.when(s == 4)
-        def _():
-            arrived(2)
+        @pl.when(s == 5)
+        def _():
             build(2, 1 - x, 2)
-
-        @pl.when(s == 5)
-        def _():
-            flatten(0)
-            build(2, x, 3)
 
         @pl.when(s < CHUNKS)
         def _():
@@ -422,10 +440,11 @@
             ig_group(1, 2, q)
 
         for lag, work in zip(LAG, (do_rs1, do_rs2, do_swap, do_ag2, do_ag1, do_onward)):
-
-            @pl.when((s >= lag) & (s < CHUNKS + lag))
+            ahead = (s == lag - 1) if lag > 1 else False
+
+            @pl.when(ahead | ((s > lag) & (s < CHUNKS + lag)))
             def _():
-                work(s - lag)
+                work(jnp.where(s < lag, 0, s - lag))
 
         return carry
 
@@ -494,8 +513,8 @@
             pltpu.VMEM((cols, in_rows, lats), f32),
             pltpu.VMEM((cols, in_rows, lats), bf16),
             pltpu.SemaphoreType.DMA((5 + 2 * CHUNKS,)),
-            pltpu.SemaphoreType.DMA((9,)),
-            pltpu.SemaphoreType.DMA((9,)),
+            pltpu.SemaphoreType.DMA((11,)),
+            pltpu.SemaphoreType.DMA((11,)),
             pltpu.SemaphoreType.DMA((3,)),
             pltpu.SemaphoreType.DMA((3,)),
             pltpu.SemaphoreType.DMA((CHUNKS, 34)),

time: 130 us -> 132 us (1.015)
  Pallas kernels: 125 us -> 127 us
    pallas_call x1, Pallas kernels: 125 us -> 127 us  [local(): pl.pallas_call(functools.partial(backward_kernel, scale), out_shape=(pltp...]
where the time goes in v7:
time: 132 us
  Pallas kernels  127 us (96%)
  local copies, waits for them, and re-layouts  3.98 us (3%)
    pallas_call x1, Pallas kernels, local(): pl.pallas_call(functools.partial(backward_kernel, scale), out_shape=(pltp...  127 us
    unnamed x2, local copies, waits for them, and re-layouts  3.98 us

profile of v7, /device:TPU:0, one launch (start us, length us, event | category | flops | bytes accessed | tf_op | source)
XLA Modules:
  0.0 131.9 jit_solution(798029337350397915)
XLA Ops:
  0.6 127.2 %backward.1 = (bf16[18,256,128]{2,1,0:T(8,128)(2,1)S(1)}, f32[1728,1024]{1,0:T(8,128)S(1)}) custom-call(bf16[18,256,128]{2,1,0:T(8,128)(2,1)} %bitcast.14, bf16[3,18,64,128]{3,2,1,0:T(8,128)(2,1)} %bitcast.15, bf16[1728,1024]{1,0:T(8,128)(2,1)} %bitcast.13), custom_call_target="tpu_custom_call" | custom-call | tf_op jit(solution)/shard_map/backward/pallas_call | solution.py:491
  127.9 1.0 copy.7
  128.9 3.0 %copy.8 = f32[3,3,3,64,1024]{4,3,2,1,0:T(8,128)} copy(f32[3,3,3,64,1024]{4,3,2,1,0:T(8,128)S(1)} %bitcast.11) | data formatting | bytes 14155776

commit v8 on v7

--- a/solution.py
+++ b/solution.py
@@ -133,16 +133,16 @@
 
         def column(m, carry):
             for lon_tap in range(3):
-                v = ext[base + d + side * cols + m - d * (lon_tap - 1)].astype(jnp.float32)
+                v = ext[base + d + side * cols + m - d * (lon_tap - 1)]
                 for lat_tap in range(3):
                     if lat_tap == 0:
-                        moved = jnp.where(lane < 128 - d, pltpu.roll(v, 128 - d, 1), 0.0)
+                        moved = pltpu.roll(v, 128 - d, 1) * (lane < 128 - d).astype(v.dtype)
                     elif lat_tap == 1:
                         moved = v
                     else:
-                        moved = jnp.where(lane >= d, pltpu.roll(v, d, 1), 0.0)
+                        moved = pltpu.roll(v, d, 1) * (lane >= d).astype(v.dtype)
                     row = slot * taps + (lat_tap * 3 + lon_tap) * out_rows
-                    stack[pl.ds(row, out_rows), aligned(m * 128, 128, 128)] = moved.astype(jnp.bfloat16)
+                    stack[pl.ds(row, out_rows), aligned(m * 128, 128, 128)] = moved
             return carry
 
         lax.fori_loop(0, cols, column, 0)
@@ -396,33 +396,26 @@
         def _():
             feat_far.wait()
             feat_on.start()
-            rests[0].wait()
-            build(0, 1 - x, 0)
+            for k in range(3):
+                if k < 2:
+                    rests[k].wait()
+                build(k, 1 - x, k)
             feat_on.wait()
             flatten(1)
 
-        @pl.when(s == 4)
-        def _():
-            rests[1].wait()
-            build(1, 1 - x, 1)
-
-        @pl.when(s == 5)
-        def _():
-            build(2, 1 - x, 2)
-
         @pl.when(s < CHUNKS)
         def _():
             do_chunk(s)
 
-        @pl.when((s >= 5) & (s < 5 + GROUPS))
-        def _():
-            far_group(s - 5)
-
-        @pl.when(s == 5 + GROUPS)
+        @pl.when((s >= 3) & (s < 3 + GROUPS))
+        def _():
+            far_group(s - 3)
+
+        @pl.when(s == 3 + GROUPS)
         def _():
             finish_far(GROUPS - 1)
 
-        @pl.when(s == 8)
+        @pl.when(s == 7)
         def _():
             load_w(xh, 1 - core).wait()
             turn(0)
@@ -432,9 +425,9 @@
             load_w(xh, core).wait()
             turn(1)
 
-        @pl.when((s >= 9) & (s < 9 + GROUPS))
-        def _():
-            q = s - 9
+        @pl.when((s >= 8) & (s < 8 + GROUPS))
+        def _():
+            q = s - 8
             ig_group(0, 0, q)
             ig_mate(0, q).start()
             ig_group(1, 2, q)

time: 132 us -> 123 us (0.932)
  Pallas kernels: 127 us -> 118 us
    pallas_call x1, Pallas kernels: 127 us -> 118 us  [local(): pl.pallas_call(functools.partial(backward_kernel, scale), out_shape=(pltp...]
where the time goes in v8:
time: 123 us
  Pallas kernels  118 us (96%)
  local copies, waits for them, and re-layouts  3.98 us (3%)
    pallas_call x1, Pallas kernels, local(): pl.pallas_call(functools.partial(backward_kernel, scale), out_shape=(pltp...  118 us
    unnamed x2, local copies, waits for them, and re-layouts  3.98 us

profile of v8, /device:TPU:0, one launch (start us, length us, event | category | flops | bytes accessed | tf_op | source)
XLA Modules:
  0.0 122.8 jit_solution(5673679300304304679)
XLA Ops:
  0.6 118.2 %backward.1 = (bf16[18,256,128]{2,1,0:T(8,128)(2,1)S(1)}, f32[1728,1024]{1,0:T(8,128)S(1)}) custom-call(bf16[18,256,128]{2,1,0:T(8,128)(2,1)} %bitcast.14, bf16[3,18,64,128]{3,2,1,0:T(8,128)(2,1)} %bitcast.15, bf16[1728,1024]{1,0:T(8,128)(2,1)} %bitcast.13), custom_call_target="tpu_custom_call" | custom-call | tf_op jit(solution)/shard_map/backward/pallas_call | solution.py:484
  118.8 1.0 copy.7
  119.8 3.0 %copy.8 = f32[3,3,3,64,1024]{4,3,2,1,0:T(8,128)} copy(f32[3,3,3,64,1024]{4,3,2,1,0:T(8,128)S(1)} %bitcast.11) | data formatting | bytes 14155776

commit v9 on v8

--- a/solution.py
+++ b/solution.py
@@ -381,9 +381,12 @@
             arrived(0)
             build(0, x, 3)
 
+        @pl.when((s >= 1) & (s <= 3))
+        def _():
+            do_rs1(s - 1)
+
         @pl.when(s == 1)
         def _():
-            do_rs1(0)
             arrived(1)
             build(1, x, 3)
 
@@ -433,11 +436,13 @@
             ig_group(1, 2, q)
 
         for lag, work in zip(LAG, (do_rs1, do_rs2, do_swap, do_ag2, do_ag1, do_onward)):
-            ahead = (s == lag - 1) if lag > 1 else False
-
-            @pl.when(ahead | ((s > lag) & (s < CHUNKS + lag)))
+            u = s - lag
+            late = (u >= 3) & (u < CHUNKS)
+            ahead = (u >= -1) & (u < 2)
+
+            @pl.when(late if lag == 1 else late | ahead)
             def _():
-                work(jnp.where(s < lag, 0, s - lag))
+                work(jnp.where(u < 2, u + 1, u))
 
         return carry
 

time: 123 us -> 126 us (1.024)
  Pallas kernels: 118 us -> 122 us
    pallas_call x1, Pallas kernels: 118 us -> 122 us  [local(): pl.pallas_call(functools.partial(backward_kernel, scale), out_shape=(pltp...]
where the time goes in v9:
time: 126 us
  Pallas kernels  122 us (97%)
  local copies, waits for them, and re-layouts  3.98 us (3%)
    pallas_call x1, Pallas kernels, local(): pl.pallas_call(functools.partial(backward_kernel, scale), out_shape=(pltp...  122 us
    unnamed x2, local copies, waits for them, and re-layouts  3.98 us

profile of v9, /device:TPU:0, one launch (start us, length us, event | category | flops | bytes accessed | tf_op | source)
XLA Modules:
  0.0 126.3 jit_solution(11172420201874991867)
XLA Ops:
  0.6 121.7 %backward.1 = (bf16[18,256,128]{2,1,0:T(8,128)(2,1)S(1)}, f32[1728,1024]{1,0:T(8,128)S(1)}) custom-call(bf16[18,256,128]{2,1,0:T(8,128)(2,1)} %bitcast.14, bf16[3,18,64,128]{3,2,1,0:T(8,128)(2,1)} %bitcast.15, bf16[1728,1024]{1,0:T(8,128)(2,1)} %bitcast.13), custom_call_target="tpu_custom_call" | custom-call | tf_op jit(solution)/shard_map/backward/pallas_call | solution.py:489
  122.3 1.0 copy.7
  123.3 3.0 %copy.8 = f32[3,3,3,64,1024]{4,3,2,1,0:T(8,128)} copy(f32[3,3,3,64,1024]{4,3,2,1,0:T(8,128)S(1)} %bitcast.11) | data formatting | bytes 14155776

commit v10 on v8

--- a/solution.py
+++ b/solution.py
@@ -51,7 +51,7 @@
     mate = (lon, xh * 2 + 1 - core)
     far = (pair + 1 - x, (1 - xh) * 2 + core)
     outer = [(lax.rem(pair + step, lons), ch) for step in (lons - 2, lons - 1, 2, 3)]
-    halo_to = [(lax.rem(pair + lons - 2 + 4 * x + i, lons), ch) for i in range(2)]
+    halo_to = [(lax.rem(pair + lons - 1 + 3 * x, lons), ch), (lax.rem(pair + lons - 2 + 5 * x, lons), ch)]
 
     def load_w(chip, who):
         columns = aligned((chip * 2 + who) * in_rows, 128, in_rows)
@@ -99,14 +99,12 @@
             )
             for i in range(2)
         ]
-        for copy in edges + [mine]:
+        for copy in (edges[0], mine):
             copy.start()
-        before = ext.at[pl.ds(base, d)]
-        after = ext.at[pl.ds(base + 2 * cols + d, d)]
-        arrivals = [
-            remote(before, before, halo_send.at[3 * k + 1], halo_recv.at[3 * k + 1], halo_to[0]),
-            remote(after, after, halo_send.at[3 * k + 1], halo_recv.at[3 * k + 2], halo_to[0]),
-        ]
+        arrivals = []
+        for i, side in enumerate((x, 1 - x)):
+            rim = ext.at[pl.ds(base + side * (2 * cols + d), d)]
+            arrivals.append(remote(rim, rim, halo_send.at[3 * k + 1 + i], halo_recv.at[3 * k + 1 + side], halo_to[i]))
         inputs.append((mine, edges, arrivals))
     rests = []
     for k, d in enumerate(DILATIONS[:2]):
@@ -120,6 +118,8 @@
             )
         )
         rests[k].start()
+    for k in range(3):
+        inputs[k][1][1].start()
     feat_mate = remote(feat_hbm, raw.at[core], feat_send.at[0], feat_recv.at[0], mate)
     feat_far = remote(feat_hbm, raw.at[2 + core], feat_send.at[1], feat_recv.at[1], far)
     feat_on = remote(raw.at[2 + core], raw.at[2 + core], feat_send.at[2], feat_recv.at[2], mate)
@@ -369,8 +369,7 @@
         mine, edges, arrivals = inputs[k]
         loads[k].wait()
         mine.wait_recv()
-        for copy in arrivals:
-            copy.wait_recv()
+        arrivals[0].wait_recv()
 
     def body(s, carry):
         @pl.when(s == 0)
@@ -399,6 +398,7 @@
             for k in range(3):
                 if k < 2:
                     rests[k].wait()
+                inputs[k][2][1].wait_recv()
                 build(k, 1 - x, k)
             feat_on.wait()
             flatten(1)

time: 123 us -> 123 us (level)
  no operation moved by 1% of the time
where the time goes in v10:
time: 123 us
  Pallas kernels  118 us (96%)
  local copies, waits for them, and re-layouts  3.98 us (3%)
    pallas_call x1, Pallas kernels, local(): pl.pallas_call(functools.partial(backward_kernel, scale), out_shape=(pltp...  118 us
    unnamed x2, local copies, waits for them, and re-layouts  3.98 us

profile of v10, /device:TPU:0, one launch (start us, length us, event | category | flops | bytes accessed | tf_op | source)
XLA Modules:
  0.0 122.8 jit_solution(17071074044555899249)
XLA Ops:
  0.6 118.2 %backward.1 = (bf16[18,256,128]{2,1,0:T(8,128)(2,1)S(1)}, f32[1728,1024]{1,0:T(8,128)S(1)}) custom-call(bf16[18,256,128]{2,1,0:T(8,128)(2,1)} %bitcast.14, bf16[3,18,64,128]{3,2,1,0:T(8,128)(2,1)} %bitcast.15, bf16[1728,1024]{1,0:T(8,128)(2,1)} %bitcast.13), custom_call_target="tpu_custom_call" | custom-call | tf_op jit(solution)/shard_map/backward/pallas_call | solution.py:484
  118.8 1.0 copy.7
  119.8 3.0 %copy.8 = f32[3,3,3,64,1024]{4,3,2,1,0:T(8,128)} copy(f32[3,3,3,64,1024]{4,3,2,1,0:T(8,128)S(1)} %bitcast.11) | data formatting | bytes 14155776
